TPU v7x, 512 devices: a whole 4x4x16 slice. The times are simulated.
512 devices in a mesh: row: 16 (over z), col: 32 (over x, y, core).
Axes of the slice: x: 4, y: 4, z: 16, core: 2. Of those that a mesh axis runs over, the one named last changes fastest.
Arguments:
- matrix: float32 [8, 16, 128, 4, 32, 128], P(None, 'row', None, None, 'col'), as said below
Outputs:
- reduced: float32 [8, 16, 128, 4, 32, 128], P(None, 'row', None, None, 'col')
Inputs may be any that keep to these rules, and one draw needn't show every extreme that they name: matrix is exactly symmetric as an 16384 x 16384 matrix.
All inputs are finite; a program needn't handle non-finite values.
Results may differ from a plain program's by a relative error of at most 0.00016.
Values sent between devices are 32-bit elements; how exact they have to be, the bound alone decides.
No kernel may reach another device: no remote copies, remote signals or barrier semaphores. Data moves between devices by JAX's collectives and lax.ppermute only.
A program may use at most 64 MiB of HBM per device.

v0:
```python
import jax
import jax.numpy as jnp
from jax import lax
from jax.sharding import PartitionSpec as P

newton_sweeps = 8


def dot(left_side, right_side, left_dim=1, right_dim=0):
    return lax.dot_general(
        left_side,
        right_side,
        (((left_dim,), (right_dim,)), ((), ())),
        precision=lax.Precision.HIGHEST,
        preferred_element_type=jnp.float32,
    )


def newton_inverse(middle):
    identity = jnp.eye(middle.shape[0], dtype=jnp.float32)
    power = identity - middle
    approx = identity + power
    for sweep_step in range(1, newton_sweeps):
        power = dot(power, power)
        approx = approx + dot(approx, power)
    return approx


def exchange(chunks, axis):
    return lax.all_to_all(chunks, axis, 0, 0)


def panel_core(gram_and_top, block):
    gram = gram_and_top[:block]
    top = gram_and_top[block:]
    identity = jnp.eye(block, dtype=jnp.float32)
    lower = jnp.linalg.cholesky(gram)
    lower_inverse = lax.linalg.triangular_solve(lower, identity, left_side=True, lower=True)
    top_q = dot(top, lower_inverse, 1, 1)
    pivot_tile = identity + top_q
    return lower_inverse, pivot_tile, newton_inverse(pivot_tile)


def local(matrix):
    tile_rows, block, tile_cols = matrix.shape[0], matrix.shape[2], matrix.shape[3]
    rows, cols = tile_rows * block, tile_cols * block
    row_count, col_count = lax.axis_size("row"), lax.axis_size("col")
    row_index, col_index = lax.axis_index("row"), lax.axis_index("col")
    spread = col_count // row_count
    part = cols // col_count
    chunk = spread * part
    small = 2 * block // col_count

    row_tiles = jnp.repeat(jnp.arange(tile_rows, dtype=jnp.int32) * row_count + row_index, block)[:, None]
    col_tiles = jnp.repeat(jnp.arange(tile_cols, dtype=jnp.int32) * col_count + col_index, block)[:, None]
    identity = jnp.eye(block, dtype=jnp.float32)

    def below(values, tiles, first):
        return jnp.where(tiles >= first, values, 0.0)

    def with_pivot(values, tiles, pivot):
        shape = (values.shape[0] // block, block, block)
        lifted = jnp.broadcast_to(identity[None], shape).reshape(values.shape)
        return values + jnp.where(tiles == pivot, lifted, 0.0)

    def chunks_of(values):
        split = values.reshape(tile_cols, spread, block // part, part, block)
        return split.transpose(0, 2, 1, 3, 4).reshape(col_count, chunk, block)

    def rows_of(chunks):
        split = chunks.reshape(tile_cols, block // part, spread, part, block)
        return split.transpose(0, 2, 1, 3, 4).reshape(rows, block)

    def share(tall, stacked):
        mine = jnp.concatenate(tall + [stacked])
        got = exchange(jnp.broadcast_to(mine[None], (row_count,) + mine.shape), "row")
        sends = []
        for index, piece in enumerate(tall):
            sends.append(jnp.broadcast_to(piece[None], (col_count, chunk, block)))
            wanted = got[:, index * chunk : (index + 1) * chunk].reshape(row_count, spread, part, block)
            sends.append(wanted.transpose(1, 0, 2, 3).reshape(col_count, part, block))
        total = got[:, len(tall) * chunk :].sum(0)
        sends.append(jnp.broadcast_to(total[None], (col_count,) + total.shape))
        got = exchange(jnp.concatenate(sends, axis=1), "col")
        results = []
        for index in range(len(tall)):
            start = index * (chunk + part)
            results.append(rows_of(got[:, start : start + chunk]))
            results.append(got[:, start + chunk : start + chunk + part].reshape(cols, block))
        results.append(got[:, len(tall) * (chunk + part) :].reshape(col_count * small, block))
        return results

    current = matrix.reshape(rows, cols)

    own_col = current[:, :block]
    masked = below(own_col, row_tiles, 1)
    gram_part = dot(masked, masked, 0, 0)
    top_part = jnp.where(row_index == 1 % row_count, own_col[:block], 0.0)
    stacked = jnp.concatenate([gram_part, top_part]).reshape(col_count, small, block)
    got = exchange(jnp.concatenate([chunks_of(own_col), stacked], axis=1), "col")
    panel_rows, panel_cols, next_rows, next_cols, gram_and_top = share(
        [got[0, :chunk], got[1, :chunk]], got[0, chunk:]
    )

    for panel_index in range(2):
        last = panel_index == 1
        first = panel_index + 1
        lower_inverse, pivot_tile, inverse_core = panel_core(gram_and_top, block)
        reflect_rows = with_pivot(dot(below(panel_rows, row_tiles, first), lower_inverse, 1, 1), row_tiles, first)
        reflect_cols = with_pivot(dot(below(panel_cols, col_tiles, first), lower_inverse, 1, 1), col_tiles, first)

        part_rows = dot(current, reflect_cols)
        pieces = [dot(reflect_rows, part_rows, 0, 0)]
        if last:
            pieces.append(jnp.zeros_like(pieces[0]))
        else:
            pieces.append(jnp.where(row_index == first % row_count, part_rows[:block], 0.0))
        stacked = jnp.concatenate(pieces).reshape(col_count, small, block)
        got = exchange(jnp.concatenate([chunks_of(part_rows), stacked], axis=1), "col").sum(0)
        w_rows, w_cols, stacked = share([got[:chunk]], got[chunk:])

        core_block = dot(dot(inverse_core, stacked[:block]), inverse_core, 1, 1)
        companion_rows = dot(w_rows, inverse_core, 1, 1) - 0.5 * dot(reflect_rows, core_block)
        companion_cols = dot(w_cols, inverse_core, 1, 1) - 0.5 * dot(reflect_cols, core_block)
        if not last:
            companion_tile = dot(stacked[block:], inverse_core, 1, 1) - 0.5 * dot(pivot_tile, core_block)
            tile_factor = jnp.concatenate([companion_tile, pivot_tile], axis=1)
            panel_cols = next_cols - dot(jnp.concatenate([reflect_cols, companion_cols], axis=1), tile_factor, 1, 1)
            masked = below(panel_cols, col_tiles, first + 1)
            gram_part = dot(masked, masked, 0, 0)
            top_part = jnp.where(col_index == (first + 1) % col_count, panel_cols[:block], 0.0)
            stacked = jnp.concatenate([gram_part, top_part]).reshape(col_count, small, block)
            total = exchange(stacked, "col").sum(0)
            copies = jnp.broadcast_to(total[None], (col_count, small, block))
            gram_and_top = exchange(copies, "col").reshape(2 * block, block)
            panel_rows = next_rows - dot(jnp.concatenate([reflect_rows, companion_rows], axis=1), tile_factor, 1, 1)
        left_factor = jnp.concatenate([reflect_rows, companion_rows], axis=1)
        right_factor = jnp.concatenate([companion_cols, reflect_cols], axis=1)
        current = current - dot(left_factor, right_factor, 1, 1)
    return current.reshape(matrix.shape)


def solution(mesh):
    in_specs = (P(None, "row", None, None, "col", None),)
    out_specs = P(None, "row", None, None, "col", None)
    return jax.shard_map(local, mesh=mesh, in_specs=in_specs, out_specs=out_specs, check_vma=False)
```

profile of v0, /device:TPU:1, one launch (start us, length us, event | category | flops | bytes accessed | tf_op | source)
XLA Modules:
  0.0 359.8 jit_solution(4725966242247270281)
XLA Ops:
  0.1 1.8 copy.147
  1.9 1.3 fusion.19
  3.4 22.5 %all_to_all.55 = f32[32,40,128]{2,1,0:T(8,128)S(1)} all-to-all(f32[32,40,128]{2,1,0:T(8,128)S(1)} %pad_maximum_fusion.5), channel_id=1, replica_groups=mesh['row'=16,'col'=32] {'col'}, dimensions={0} | all-to-all | bytes 1310720 | tf_op jit(solution)/shard_map/all_to_all | solution.py:30
  26.8 13.7 %all-to-all-start.1 = ((f32[16,72,128]{2,1,0:T(8,128)}), f32[16,72,128]{2,1,0:T(8,128)S(1)}, u32[]{:S(2)}, u32[]{:S(2)}) async-start(f32[16,72,128]{2,1,0:T(8,128)} %broadcast_in_dim.190), calls=%async_computation.1 | async-start | bytes 1179648 | tf_op jit(solution)/shard_map/all_to_all | solution.py:30
  41.5 26.2 %all-to-all-done.1 = f32[16,72,128]{2,1,0:T(8,128)S(1)} async-done(((f32[16,72,128]{2,1,0:T(8,128)}), f32[16,72,128]{2,1,0:T(8,128)S(1)}, u32[]{:S(2)}, u32[]{:S(2)}) %all-to-all-start.1) | async-done | bytes 589856 | tf_op jit(solution)/shard_map/all_to_all | solution.py:30
  70.8 10.1 %all-to-all-start.2 = ((f32[32,104,128]{2,1,0:T(8,128)}), f32[32,104,128]{2,1,0:T(8,128)S(1)}, u32[]{:S(2)}, u32[]{:S(2)}) async-start(f32[32,104,128]{2,1,0:T(8,128)} %broadcast_dynamic-update-slice_fusion.2), calls=%async_computation.2 | async-start | bytes 3407872 | tf_op jit(solution)/shard_map/all_to_all | solution.py:30
  82.1 1.3 bitcast_select_fusion
  83.7 21.3 %all-to-all-done.2 = f32[32,104,128]{2,1,0:T(8,128)S(1)} async-done(((f32[32,104,128]{2,1,0:T(8,128)}), f32[32,104,128]{2,1,0:T(8,128)S(1)}, u32[]{:S(2)}, u32[]{:S(2)}) %all-to-all-start.2) | async-done | bytes 1703968 | tf_op jit(solution)/shard_map/all_to_all | solution.py:30
  105.2 11.7 %cholesky.44 = f32[128,128]{1,0:T(8,128)S(1)} custom-call(f32[128,128]{1,0:T(8,128)S(1)} %fusion.42), custom_call_target="Cholesky" | custom-call | tf_op jit(solution)/shard_map/jit(cholesky)/cholesky | solution.py:37
  118.3 9.8 %custom-call.6 = f32[1,128,128]{1,2,0:T(8,128)S(1)} custom-call(f32[1,128,128]{2,1,0:T(8,128)S(1)} %fusion.34), custom_call_target="InvertDiagBlocksLowerTriangular" | custom-call | tf_op jit(solution)/shard_map/triangular_solve/custom-call.0 | solution.py:38
  130.2 1.0 fusion.55
  131.2 1.0 bitcast_select_fusion.2
  132.2 1.8 fusion.54
  134.5 2.3 fusion.53
  136.8 1.0 copy.80
  137.8 1.8 convolution_add_fusion.1
  139.7 1.0 fusion.57
  141.7 4.5 %all-to-all-start.3 = ((f32[32,40,128]{2,1,0:T(8,128)}), f32[32,40,128]{2,1,0:T(8,128)S(1)}, u32[]{:S(2)}, u32[]{:S(2)}) async-start(f32[32,40,128]{2,1,0:T(8,128)} %pad_maximum_fusion.6), calls=%async_computation.3 | async-start | bytes 1310720 | tf_op jit(solution)/shard_map/all_to_all | solution.py:30
  146.1 1.1 fusion.58
  147.3 1.8 convolution_add_fusion.17
  149.9 9.3 %all-to-all-done.3 = f32[32,40,128]{2,1,0:T(8,128)S(1)} async-done(((f32[32,40,128]{2,1,0:T(8,128)}), f32[32,40,128]{2,1,0:T(8,128)S(1)}, u32[]{:S(2)}, u32[]{:S(2)}) %all-to-all-start.3) | async-done | bytes 655392 | tf_op jit(solution)/shard_map/all_to_all | solution.py:30
  159.8 1.5 broadcast_in_dim.203
  161.3 5.6 %all-to-all-start.4 = ((f32[16,40,128]{2,1,0:T(8,128)}), f32[16,40,128]{2,1,0:T(8,128)S(1)}, u32[]{:S(2)}, u32[]{:S(2)}) async-start(f32[16,40,128]{2,1,0:T(8,128)} %broadcast_in_dim.203), calls=%async_computation.4 | async-start | bytes 655360 | tf_op jit(solution)/shard_map/all_to_all | solution.py:30
  166.9 1.2 convolution_add_fusion.16
  168.1 1.9 copy.95
  171.2 12.7 %all-to-all-done.4 = f32[16,40,128]{2,1,0:T(8,128)S(1)} async-done(((f32[16,40,128]{2,1,0:T(8,128)}), f32[16,40,128]{2,1,0:T(8,128)S(1)}, u32[]{:S(2)}, u32[]{:S(2)}) %all-to-all-start.4) | async-done | bytes 327712 | tf_op jit(solution)/shard_map/all_to_all | solution.py:30
  184.1 1.0 pad_maximum_fusion.1
  185.1 9.4 %all-to-all-start.5 = ((f32[32,56,128]{2,1,0:T(8,128)}), f32[32,56,128]{2,1,0:T(8,128)}, u32[]{:S(2)}, u32[]{:S(2)}) async-start(f32[32,56,128]{2,1,0:T(8,128)} %pad_maximum_fusion.1), calls=%async_computation.5 | async-start | bytes 1835008 | tf_op jit(solution)/shard_map/all_to_all | solution.py:30
  195.6 14.6 %all-to-all-done.5 = f32[32,56,128]{2,1,0:T(8,128)} async-done(((f32[32,56,128]{2,1,0:T(8,128)}), f32[32,56,128]{2,1,0:T(8,128)}, u32[]{:S(2)}, u32[]{:S(2)}) %all-to-all-start.5) | async-done | bytes 917536 | tf_op jit(solution)/shard_map/all_to_all | solution.py:30
  210.2 1.1 fusion.38
  211.5 1.1 slice.186
  213.2 1.2 fusion.37
  215.3 1.0 slice.189
  219.8 4.3 %all-to-all-start.6 = ((f32[32,8,128]{2,1,0:T(8,128)}), f32[32,8,128]{2,1,0:T(8,128)}, u32[]{:S(2)}, u32[]{:S(2)}) async-start(f32[32,8,128]{2,1,0:T(8,128)} %maximum_bitcast_fusion.2), calls=%async_computation.6 | async-start | bytes 262144 | tf_op jit(solution)/shard_map/all_to_all | solution.py:30
  224.2 4.1 %convolution_subtract_fusion.1 = f32[1024,512]{1,0:T(8,128)} fusion(f32[1024,128]{1,0:T(8,128)S(1)} %fusion.2, f32[1024,128]{1,0:T(8,128)S(1)} %convolution_add_fusion.1, f32[512,128]{1,0:T(8,128)S(1)} %convolution_add_fusion.3, f32[512,128]{1,0:T(8,128)} %copy-done.8, f32[128,8,4,128]{3,2,1,0:T(4,128)S(1)} %bitcast.235), kind=kOutput, calls=%fused_computation.2 | convolution fusion | flops 1611530240 | bytes 5767168 | tf_op jit(solution)/shard_map/dot_general | solution.py:10
  228.3 3.4 all-to-all-done.6
  233.4 5.1 %all-to-all-start.7 = ((f32[32,8,128]{2,1,0:T(8,128)}), f32[32,8,128]{2,1,0:T(8,128)}, u32[]{:S(2)}, u32[]{:S(2)}) async-start(f32[32,8,128]{2,1,0:T(8,128)} %broadcast_in_dim.209), calls=%async_computation.7 | async-start | bytes 262144 | tf_op jit(solution)/shard_map/all_to_all | solution.py:30
  238.5 2.8 fusion
  241.3 4.8 %all-to-all-done.7 = f32[32,8,128]{2,1,0:T(8,128)} async-done(((f32[32,8,128]{2,1,0:T(8,128)}), f32[32,8,128]{2,1,0:T(8,128)}, u32[]{:S(2)}, u32[]{:S(2)}) %all-to-all-start.7) | async-done | bytes 131104 | tf_op jit(solution)/shard_map/all_to_all | solution.py:30
  247.9 11.7 %cholesky.55 = f32[128,128]{1,0:T(8,128)S(1)} custom-call(f32[128,128]{1,0:T(8,128)S(1)} %fusion.40), custom_call_target="Cholesky" | custom-call | tf_op jit(solution)/shard_map/jit(cholesky)/cholesky | solution.py:37
  261.0 9.8 %custom-call.7 = f32[1,128,128]{1,2,0:T(8,128)S(1)} custom-call(f32[1,128,128]{2,1,0:T(8,128)S(1)} %fusion.35), custom_call_target="InvertDiagBlocksLowerTriangular" | custom-call | tf_op jit(solution)/shard_map/triangular_solve/custom-call.0 | solution.py:38
  271.1 1.4 convolution_add_fusion.2
  272.5 1.1 fusion.5
  274.6 1.8 convolution_add_fusion
  276.4 1.8 fusion.67
  278.2 1.0 fusion.68
  280.1 4.1 %all-to-all-start.8 = ((f32[32,40,128]{2,1,0:T(8,128)}), f32[32,40,128]{2,1,0:T(8,128)S(1)}, u32[]{:S(2)}, u32[]{:S(2)}) async-start(f32[32,40,128]{2,1,0:T(8,128)} %pad_maximum_fusion.7), calls=%async_computation.8 | async-start | bytes 1310720 | tf_op jit(solution)/shard_map/all_to_all | solution.py:30
  284.2 1.8 convolution_add_fusion.10
  286.0 1.1 fusion.70
  288.6 8.6 %all-to-all-done.8 = f32[32,40,128]{2,1,0:T(8,128)S(1)} async-done(((f32[32,40,128]{2,1,0:T(8,128)}), f32[32,40,128]{2,1,0:T(8,128)S(1)}, u32[]{:S(2)}, u32[]{:S(2)}) %all-to-all-start.8) | async-done | bytes 655392 | tf_op jit(solution)/shard_map/all_to_all | solution.py:30
  297.9 1.5 broadcast_in_dim.215
  299.5 5.4 %all-to-all-start.9 = ((f32[16,40,128]{2,1,0:T(8,128)}), f32[16,40,128]{2,1,0:T(8,128)S(1)}, u32[]{:S(2)}, u32[]{:S(2)}) async-start(f32[16,40,128]{2,1,0:T(8,128)} %broadcast_in_dim.215), calls=%async_computation.9 | async-start | bytes 655360 | tf_op jit(solution)/shard_map/all_to_all | solution.py:30
  304.9 1.2 convolution_add_fusion.9
  306.1 1.1 fusion.72
  307.3 1.1 convolution_add_fusion.8
  309.1 12.8 %all-to-all-done.9 = f32[16,40,128]{2,1,0:T(8,128)S(1)} async-done(((f32[16,40,128]{2,1,0:T(8,128)}), f32[16,40,128]{2,1,0:T(8,128)S(1)}, u32[]{:S(2)}, u32[]{:S(2)}) %all-to-all-start.9) | async-done | bytes 327712 | tf_op jit(solution)/shard_map/all_to_all | solution.py:30
  322.1 1.0 pad_maximum_fusion.2
  323.1 9.4 %all-to-all-start.10 = ((f32[32,56,128]{2,1,0:T(8,128)}), f32[32,56,128]{2,1,0:T(8,128)}, u32[]{:S(2)}, u32[]{:S(2)}) async-start(f32[32,56,128]{2,1,0:T(8,128)} %pad_maximum_fusion.2), calls=%async_computation.10 | async-start | bytes 1835008 | tf_op jit(solution)/shard_map/all_to_all | solution.py:30
  333.6 14.6 %all-to-all-done.10 = f32[32,56,128]{2,1,0:T(8,128)} async-done(((f32[32,56,128]{2,1,0:T(8,128)}), f32[32,56,128]{2,1,0:T(8,128)}, u32[]{:S(2)}, u32[]{:S(2)}) %all-to-all-start.10) | async-done | bytes 917536 | tf_op jit(solution)/shard_map/all_to_all | solution.py:30
  348.2 1.1 fusion.36
  349.5 1.1 slice.198
  351.3 1.0 slice.201
  353.5 3.2 convolution_subtract_fusion
  356.7 2.9 reshape.252
  (147 shorter events, 33.7 us)
Async XLA Ops:
  26.8 40.9 %all-to-all-start.1 = ((f32[16,72,128]{2,1,0:T(8,128)}), f32[16,72,128]{2,1,0:T(8,128)S(1)}, u32[]{:S(2)}, u32[]{:S(2)}) async-start(f32[16,72,128]{2,1,0:T(8,128)} %broadcast_in_dim.190), calls=%async_computation.1 | async-start | bytes 1179648 | tf_op jit(solution)/shard_map/all_to_all | solution.py:30
  70.8 34.2 %all-to-all-start.2 = ((f32[32,104,128]{2,1,0:T(8,128)}), f32[32,104,128]{2,1,0:T(8,128)S(1)}, u32[]{:S(2)}, u32[]{:S(2)}) async-start(f32[32,104,128]{2,1,0:T(8,128)} %broadcast_dynamic-update-slice_fusion.2), calls=%async_computation.2 | async-start | bytes 3407872 | tf_op jit(solution)/shard_map/all_to_all | solution.py:30
  105.0 26.1 %copy-start.2 = (f32[32,104,128]{2,1,0:T(8,128)}, f32[32,104,128]{2,1,0:T(8,128)S(1)}, u32[]{:S(2)}) copy-start(f32[32,104,128]{2,1,0:T(8,128)S(1)} %all-to-all-done.2) | copy-start | bytes 5111812
  128.6 0.6 copy-start.6
  131.1 3.4 copy-start
  137.8 2.8 copy-start.5
  141.7 17.5 %all-to-all-start.3 = ((f32[32,40,128]{2,1,0:T(8,128)}), f32[32,40,128]{2,1,0:T(8,128)S(1)}, u32[]{:S(2)}, u32[]{:S(2)}) async-start(f32[32,40,128]{2,1,0:T(8,128)} %pad_maximum_fusion.6), calls=%async_computation.3 | async-start | bytes 1310720 | tf_op jit(solution)/shard_map/all_to_all | solution.py:30
  147.3 1.8 copy-start.12
  159.8 10.2 %copy-start.10 = (f32[128,128]{1,0:T(8,128)S(1)}, f32[128,128]{1,0:T(8,128)}, u32[]{:S(2)}) copy-start(f32[128,128]{1,0:T(8,128)} %fusion.59) | copy-start | bytes 196612
  161.3 22.7 %slice-start = ((f32[40,128]{1,0:T(8,128)}), f32[32,128]{1,0:T(8,128)S(1)}, s32[]{:S(2)}) async-start(f32[40,128]{1,0:T(8,128)} %reduce_sum.55), calls=%async_computation.11 | async-start | bytes 32768 | tf_op jit(solution)/shard_map/slice | solution.py:120
  161.3 22.6 %all-to-all-start.4 = ((f32[16,40,128]{2,1,0:T(8,128)}), f32[16,40,128]{2,1,0:T(8,128)S(1)}, u32[]{:S(2)}, u32[]{:S(2)}) async-start(f32[16,40,128]{2,1,0:T(8,128)} %broadcast_in_dim.203), calls=%async_computation.4 | async-start | bytes 655360 | tf_op jit(solution)/shard_map/all_to_all | solution.py:30
  185.1 25.1 %all-to-all-start.5 = ((f32[32,56,128]{2,1,0:T(8,128)}), f32[32,56,128]{2,1,0:T(8,128)}, u32[]{:S(2)}, u32[]{:S(2)}) async-start(f32[32,56,128]{2,1,0:T(8,128)} %pad_maximum_fusion.1), calls=%async_computation.5 | async-start | bytes 1835008 | tf_op jit(solution)/shard_map/all_to_all | solution.py:30
  195.0 19.4 %copy-start.7 = (f32[128,128]{0,1:T(8,128)S(1)}, f32[128,128]{0,1:T(8,128)}, u32[]{:S(2)}) copy-start(f32[128,128]{0,1:T(8,128)} %copy-done.6) | copy-start | bytes 196612
  213.2 3.8 %copy-start.13 = (f32[32,16,128]{2,1,0:T(8,128)S(1)}, f32[32,16,128]{2,1,0:T(8,128)}, u32[]{:S(2)}) copy-start(f32[32,16,128]{2,1,0:T(8,128)} %get-tuple-element.6) | copy-start | bytes 786436
  214.7 2.9 copy-start.14
  217.0 2.1 copy-start.8
  217.7 0.7 copy-start.3
  219.8 12.0 %all-to-all-start.6 = ((f32[32,8,128]{2,1,0:T(8,128)}), f32[32,8,128]{2,1,0:T(8,128)}, u32[]{:S(2)}, u32[]{:S(2)}) async-start(f32[32,8,128]{2,1,0:T(8,128)} %maximum_bitcast_fusion.2), calls=%async_computation.6 | async-start | bytes 262144 | tf_op jit(solution)/shard_map/all_to_all | solution.py:30
  224.1 14.3 %copy-start.15 = (f32[128,128]{0,1:T(8,128)S(1)}, f32[128,128]{0,1:T(8,128)}, u32[]{:S(2)}) copy-start(f32[128,128]{0,1:T(8,128)} %copy-done.14) | copy-start | bytes 196612
  228.3 42.8 %copy-start.4 = (f32[512,128]{1,0:T(8,128)S(1)}, f32[512,128]{1,0:T(8,128)}, u32[]{:S(2)}) copy-start(f32[512,128]{1,0:T(8,128)} %copy-done.3) | copy-start | bytes 786436
  233.4 12.8 %all-to-all-start.7 = ((f32[32,8,128]{2,1,0:T(8,128)}), f32[32,8,128]{2,1,0:T(8,128)}, u32[]{:S(2)}, u32[]{:S(2)}) async-start(f32[32,8,128]{2,1,0:T(8,128)} %broadcast_in_dim.209), calls=%async_computation.7 | async-start | bytes 262144 | tf_op jit(solution)/shard_map/all_to_all | solution.py:30
  241.3 35.0 %copy-start.1 = (f32[1024,512]{1,0:T(8,128)S(1)}, f32[1024,512]{1,0:T(8,128)}, u32[]{:S(2)}) copy-start(f32[1024,512]{1,0:T(8,128)} %convolution_subtract_fusion.1) | copy-start | bytes 6291460
  273.6 0.9 copy-start.9
  280.1 17.1 %all-to-all-start.8 = ((f32[32,40,128]{2,1,0:T(8,128)}), f32[32,40,128]{2,1,0:T(8,128)S(1)}, u32[]{:S(2)}, u32[]{:S(2)}) async-start(f32[32,40,128]{2,1,0:T(8,128)} %pad_maximum_fusion.7), calls=%async_computation.8 | async-start | bytes 1310720 | tf_op jit(solution)/shard_map/all_to_all | solution.py:30
  287.2 0.6 copy-start.11
  297.9 24.1 %slice-start.1 = ((f32[40,128]{1,0:T(8,128)}), f32[32,128]{1,0:T(8,128)S(1)}, s32[]{:S(2)}) async-start(f32[40,128]{1,0:T(8,128)} %reduce_sum.58), calls=%async_computation.12 | async-start | bytes 32768 | tf_op jit(solution)/shard_map/slice | solution.py:120
  299.5 22.5 %all-to-all-start.9 = ((f32[16,40,128]{2,1,0:T(8,128)}), f32[16,40,128]{2,1,0:T(8,128)S(1)}, u32[]{:S(2)}, u32[]{:S(2)}) async-start(f32[16,40,128]{2,1,0:T(8,128)} %broadcast_in_dim.215), calls=%async_computation.9 | async-start | bytes 655360 | tf_op jit(solution)/shard_map/all_to_all | solution.py:30
  323.1 25.1 %all-to-all-start.10 = ((f32[32,56,128]{2,1,0:T(8,128)}), f32[32,56,128]{2,1,0:T(8,128)}, u32[]{:S(2)}, u32[]{:S(2)}) async-start(f32[32,56,128]{2,1,0:T(8,128)} %pad_maximum_fusion.2), calls=%async_computation.10 | async-start | bytes 1835008 | tf_op jit(solution)/shard_map/all_to_all | solution.py:30
where the time goes:
time: 365 us; the launch traced here: 360 us
  waiting for transfers between devices  128 us (35%)
  starting transfers between devices  71.7 us (20%)
  other arithmetic  56.9 us (16%)
  matrix products  52.1 us (14%)
  local copies, waits for them, and re-layouts  27.1 us (7%)
  blocking collectives  22.5 us (6%)
    all_to_all x10, waiting for transfers between devices, exchange(): return lax.all_to_all(chunks, axis, 0, 0)  128 us
    all_to_all x10, starting transfers between devices, exchange(): return lax.all_to_all(chunks, axis, 0, 0)  71.7 us
    dot_general x58, matrix products, dot(): lax.dot_general(left_side, right_side, (((left_dim,), (right_dim,)), ((),...  51.5 us
    another operation x6, other arithmetic, panel_core(): lower = jnp.linalg.cholesky(gram)  24.9 us
    all_to_all x1, blocking collectives, exchange(): return lax.all_to_all(chunks, axis, 0, 0)  22.5 us
    another operation x4, other arithmetic, panel_core(): lax.linalg.triangular_solve(lower, identity, left_side=True, lower=True)  20.9 us
  transfers between devices with their start and end apart: 10, of which 10 were waited for; matrix products, arithmetic and copies ran while one was open for 8% of the time, Pallas kernels for 0%

commit v1 on v0

v1 whole, which is shorter than its diff:
```python
import functools

import jax
import jax.numpy as jnp
from jax import lax
from jax.experimental import pallas as pl
from jax.experimental.pallas import tpu as pltpu
from jax.sharding import PartitionSpec as P

newton_sweeps = 8
pivot_group = 4


def dot(left_side, right_side, left_dim=1, right_dim=0):
    return lax.dot_general(
        left_side,
        right_side,
        (((left_dim,), (right_dim,)), ((), ())),
        precision=lax.Precision.HIGHEST,
        preferred_element_type=jnp.float32,
    )


def halves_of(values):
    high = values.astype(jnp.bfloat16)
    return high, (values - high.astype(jnp.float32)).astype(jnp.bfloat16)


def wide_dot(left_side, right_side, right_dim=0):
    left_high, left_low = halves_of(left_side)
    right_high, right_low = halves_of(right_side)

    def product(first, second):
        return lax.dot_general(
            first, second, (((1,), (right_dim,)), ((), ())), preferred_element_type=jnp.float32
        )

    return product(left_high, right_high) + (product(left_high, right_low) + product(left_low, right_high))


def newton_inverse(middle):
    identity = jnp.eye(middle.shape[0], dtype=jnp.float32)
    power = identity - middle
    approx = identity + power
    for sweep_step in range(1, newton_sweeps):
        power = dot(power, power)
        approx = approx + dot(approx, power)
    return approx


def exchange(chunks, axis):
    return lax.all_to_all(chunks, axis, 0, 0)


def eye_of(block):
    row = lax.broadcasted_iota(jnp.int32, (block, block), 0)
    lane = lax.broadcasted_iota(jnp.int32, (block, block), 1)
    return jnp.where(row == lane, 1.0, 0.0).astype(jnp.float32)


def factor_inverse(gram, scratch):
    block = gram.shape[0]
    tiles = block // 8
    shape = (8, block)
    lane = lax.broadcasted_iota(jnp.int32, shape, 1)
    sub = lax.broadcasted_iota(jnp.int32, shape, 0)
    left = [gram[8 * b : 8 * b + 8] for b in range(tiles)]
    right = [jnp.where(lane == sub + 8 * b, 1.0, 0.0).astype(jnp.float32) for b in range(tiles)]
    members = range(pivot_group)
    for start in range(0, block, pivot_group):
        home, top = start // 8, start % 8
        pivots = [jnp.broadcast_to(left[home][top + i : top + i + 1], shape) for i in members]
        shadows = [jnp.broadcast_to(right[home][top + i : top + i + 1], shape) for i in members]
        corner = [
            [
                jnp.broadcast_to(left[home][top + i : top + i + 1, start + m : start + m + 1], shape)
                for m in members
            ]
            for i in members
        ]
        inverse = []
        for i in members:
            root = lax.rsqrt(corner[i][i])
            inverse.append(root * root)
            scratch[start + i : start + i + 1, :] = (shadows[i] * root)[0:1]
            for j in range(i + 1, pivot_group):
                factor = corner[j][i] * inverse[i]
                pivots[j] = pivots[j] - factor * pivots[i]
                shadows[j] = shadows[j] - factor * shadows[i]
                for m in range(i + 1, pivot_group):
                    corner[j][m] = corner[j][m] - factor * corner[i][m]
        for b in range((start + pivot_group) // 8, tiles):
            column = [jnp.broadcast_to(left[b][:, start + i : start + i + 1], shape) for i in members]
            for i in members:
                factor = column[i] * inverse[i]
                for m in range(i + 1, pivot_group):
                    column[m] = column[m] - factor * corner[i][m]
                left[b] = left[b] - factor * pivots[i]
                right[b] = right[b] - factor * shadows[i]
    return scratch[...]


def launch(body, shapes, place, *operands, scratch=None):
    outs = [jax.ShapeDtypeStruct(shape, jnp.float32) for shape in shapes]

    def kernel(*refs):
        extra = refs[len(refs) - 1 :] if scratch else ()
        inputs = refs[1 : 1 + len(operands)]
        results = body(refs[0], *[ref[...] for ref in inputs], *extra)
        for ref, value in zip(refs[1 + len(operands) : 1 + len(operands) + len(outs)], results, strict=True):
            ref[...] = value

    vmem = pl.BlockSpec(memory_space=pltpu.VMEM)
    return pl.pallas_call(
        kernel,
        out_shape=outs,
        in_specs=[pl.BlockSpec(memory_space=pltpu.SMEM)] + [vmem] * len(operands),
        out_specs=[vmem] * len(outs),
        scratch_shapes=[pltpu.VMEM(scratch, jnp.float32)] if scratch else [],
    )(place, *operands)


def first_tile(values, block, change):
    return jnp.concatenate([change(values[:block]), values[block:]])


def keep_from(values, block, index, first):
    return first_tile(values, block, lambda tile: tile * jnp.where(index >= first, 1.0, 0.0))


def front_body(place, stacked, panel_even, panel_odd, panel_cols, current, scratch, *, first, last, sizes):
    block, spread, part, col_count, small, tile_cols = sizes
    identity = eye_of(block)
    lower_inverse = factor_inverse(stacked[:block], scratch)
    pivot_tile = identity + dot(stacked[block:], lower_inverse, 1, 1)

    def reflect(panel, index):
        q = dot(keep_from(panel, block, index, first), lower_inverse, 1, 1)
        return first_tile(q, block, lambda tile: tile + identity * jnp.where(index == first, 1.0, 0.0))

    cols = reflect(panel_cols, place[1])
    even = reflect(panel_even, place[0])
    odd = dot(panel_odd, lower_inverse, 1, 1)
    product = wide_dot(current, cols)
    tiles = [product[block * t : block * t + block] for t in range(spread * tile_cols)]
    sums = [jnp.concatenate(tiles[h::spread]) for h in range(spread)]
    cross = dot(even.T, sums[0]) + dot(odd.T, sums[1])
    if last:
        pivot_rows = jnp.zeros_like(cross)
    else:
        pivot_rows = tiles[0] * jnp.where(place[0] == first, 1.0, 0.0)
    little = jnp.concatenate([cross, pivot_rows]).reshape(col_count, small, block)
    send = jnp.concatenate([each.reshape(col_count, part, block) for each in sums] + [little], axis=1)
    return send, even, odd, cols, pivot_tile


def split_shared(got, start, sizes):
    block, spread, part, col_count, small, tile_cols = sizes
    pieces = [
        got[:, start + part * h : start + part * h + part].reshape(col_count * part, block) for h in range(spread + 1)
    ]
    return pieces[:spread], pieces[spread]


def companions(got, inverse_core, even, odd, cols, core_block, sizes):
    (w_even, w_odd), w_cols = split_shared(got, 0, sizes)
    pairs = ((w_even, even), (w_odd, odd), (w_cols, cols))
    return [dot(w, inverse_core, 1, 1) - 0.5 * dot(v, core_block) for w, v in pairs]


def middle_body(place, got, inverse_core, cols, pivot_tile, shared, *, first, sizes):
    block, spread, part, col_count, small, tile_cols = sizes
    little = got[:, (spread + 1) * part :].reshape(col_count * small, block)
    core_block = dot(dot(inverse_core, little[:block]), inverse_core, 1, 1)
    w_cols = split_shared(got, 0, sizes)[1]
    companion = dot(w_cols, inverse_core, 1, 1) - 0.5 * dot(cols, core_block)
    companion_tile = dot(little[block:], inverse_core, 1, 1) - 0.5 * dot(pivot_tile, core_block)
    panel = split_shared(shared, (spread + 1) * part, sizes)[1]
    panel = panel - (dot(cols, companion_tile, 1, 1) + dot(companion, pivot_tile, 1, 1))
    masked = keep_from(panel, block, place[1], first + 1)
    gram = dot(masked.T, masked)
    top = panel[:block] * jnp.where(place[1] == first + 1, 1.0, 0.0)
    send = jnp.concatenate([gram, top]).reshape(col_count, small, block)
    return send, core_block, companion_tile, panel


def update_tiles(current, even, odd, even_z, odd_z, cols, cols_z, sizes):
    block, spread, part, col_count, small, tile_cols = sizes
    right = jnp.concatenate([cols_z, cols], axis=1)
    lefts = [jnp.concatenate([even, even_z], axis=1), jnp.concatenate([odd, odd_z], axis=1)]
    pieces = [lefts[h][block * u : block * u + block] for u in range(tile_cols) for h in range(spread)]
    return current - wide_dot(jnp.concatenate(pieces), right, 1)


def between_body(place, current, got, inverse_core, core_block, even, odd, cols, companion_tile, pivot_tile, shared, *, sizes):
    block, spread, part, col_count, small, tile_cols = sizes
    even_z, odd_z, cols_z = companions(got, inverse_core, even, odd, cols, core_block, sizes)
    (next_even, next_odd), unused = split_shared(shared, (spread + 1) * part, sizes)
    panels = [
        values - (dot(v, companion_tile, 1, 1) + dot(z, pivot_tile, 1, 1))
        for values, v, z in ((next_even, even, even_z), (next_odd, odd, odd_z))
    ]
    return update_tiles(current, even, odd, even_z, odd_z, cols, cols_z, sizes), panels[0], panels[1]


def final_body(place, current, got, inverse_core, even, odd, cols, *, sizes):
    block, spread, part, col_count, small, tile_cols = sizes
    cross = got[:, (spread + 1) * part :].reshape(col_count * small, block)[:block]
    core_block = dot(dot(inverse_core, cross), inverse_core, 1, 1)
    even_z, odd_z, cols_z = companions(got, inverse_core, even, odd, cols, core_block, sizes)
    return (update_tiles(current, even, odd, even_z, odd_z, cols, cols_z, sizes),)


def local(matrix):
    tile_rows, block, tile_cols = matrix.shape[0], matrix.shape[2], matrix.shape[3]
    rows, cols = tile_rows * block, tile_cols * block
    row_count, col_count = lax.axis_size("row"), lax.axis_size("col")
    row_index, col_index = lax.axis_index("row"), lax.axis_index("col")
    spread = col_count // row_count
    part = cols // col_count
    chunk = spread * part
    small = 2 * block // col_count
    sizes = (block, spread, part, col_count, small, tile_cols)
    place = jnp.stack([row_index, col_index]).astype(jnp.int32)
    tall = (cols, block)
    tile = (block, block)

    def chunks_of(values):
        split = values.reshape(tile_cols, spread, block // part, part, block)
        return split.transpose(0, 2, 1, 3, 4).reshape(col_count, chunk, block)

    def share(mine, count):
        got = exchange(jnp.broadcast_to(mine[None], (row_count,) + mine.shape), "row")
        sends = []
        for index in range(count):
            piece = mine[index * chunk : (index + 1) * chunk]
            sends.append(jnp.broadcast_to(piece[None], (col_count, chunk, block)))
            wanted = got[:, index * chunk : (index + 1) * chunk].reshape(row_count, spread, part, block)
            sends.append(wanted.transpose(1, 0, 2, 3).reshape(col_count, part, block))
        total = got[:, count * chunk :].sum(0)
        sends.append(jnp.broadcast_to(total[None], (col_count,) + total.shape))
        return exchange(jnp.concatenate(sends, axis=1), "col")

    current = matrix.reshape(rows, cols)

    own_col = current[:, :block]
    tile_ids = jnp.repeat(jnp.arange(tile_rows, dtype=jnp.int32) * row_count + row_index, block)[:, None]
    masked = jnp.where(tile_ids >= 1, own_col, 0.0)
    gram_part = dot(masked, masked, 0, 0)
    top_part = jnp.where(row_index == 1, own_col[:block], 0.0)
    stacked = jnp.concatenate([gram_part, top_part]).reshape(col_count, small, block)
    got = exchange(jnp.concatenate([chunks_of(own_col), stacked], axis=1), "col")
    shared = share(jnp.concatenate([got[0, :chunk], got[1, :chunk], got[0, chunk:]]), 2)
    stacked = shared[:, 2 * (chunk + part) :].reshape(2 * block, block)
    even, odd = (shared[:, part * h : part * h + part].reshape(cols, block) for h in range(spread))
    panel_cols = shared[:, chunk : chunk + part].reshape(cols, block)

    for panel_index in range(2):
        last = panel_index == 1
        first = panel_index + 1
        send, even, odd, panel_cols, pivot_tile = launch(
            functools.partial(front_body, first=first, last=last, sizes=sizes),
            [(col_count, chunk + small, block), tall, tall, tall, tile],
            place, stacked, even, odd, panel_cols, current, scratch=tile,
        )
        inverse_core = newton_inverse(pivot_tile)
        got = share(exchange(send, "col").sum(0), 1)
        if last:
            (current,) = launch(
                functools.partial(final_body, sizes=sizes),
                [(rows, cols)],
                place, current, got, inverse_core, even, odd, panel_cols,
            )
            break
        send, core_block, companion_tile, next_cols = launch(
            functools.partial(middle_body, first=first, sizes=sizes),
            [(col_count, small, block), tile, tile, tall],
            place, got, inverse_core, panel_cols, pivot_tile, shared,
        )
        total = exchange(send, "col").sum(0)
        copies = jnp.broadcast_to(total[None], (col_count, small, block))
        stacked = exchange(copies, "col").reshape(2 * block, block)
        current, even, odd = launch(
            functools.partial(between_body, sizes=sizes),
            [(rows, cols), tall, tall],
            place, current, got, inverse_core, core_block, even, odd, panel_cols, companion_tile, pivot_tile, shared,
        )
        panel_cols = next_cols
    return current.reshape(matrix.shape)


def solution(mesh):
    in_specs = (P(None, "row", None, None, "col", None),)
    out_specs = P(None, "row", None, None, "col", None)
    return jax.shard_map(local, mesh=mesh, in_specs=in_specs, out_specs=out_specs, check_vma=False)
```

time: 365 us -> 307 us (0.84); the launches traced: 360 us -> 306 us
  other arithmetic: 56.9 us -> 2.85 us
  Pallas kernels: 0 us -> 41.9 us
  matrix products: 52.1 us -> 11.8 us
  blocking collectives: 22.5 us -> 34 us
  local copies, waits for them, and re-layouts: 27.1 us -> 16.2 us
  starting transfers between devices: 71.7 us -> 67 us
    another operation x10 -> x1, other arithmetic: 45.8 us -> 0.59 us  [local(): place = jnp.stack([row_index, col_index]).astype(jnp.int32)]
    pallas_call x0 -> x5, Pallas kernels: none -> 41.9 us  [launch(): pl.pallas_call(kernel, out_shape=outs, in_specs=[pl.BlockSpec(memory_spac...]
    dot_general x58 -> x29, matrix products: 51.5 us -> 11.8 us  [dot(): lax.dot_general(left_side, right_side, (((left_dim,), (right_dim,)), ((),...]
    all_to_all x1 -> x2, blocking collectives: 22.5 us -> 34 us  [exchange(): return lax.all_to_all(chunks, axis, 0, 0)]
    slice x14 -> x3, local copies, waits for them, and re-layouts: 7.88 us -> 0.92 us  [the longest x1 0.91 us: local(): panel_cols = shared[:, chunk:chunk + part].reshape(cols, block)]
    all_to_all x10 -> x9, starting transfers between devices: 71.7 us -> 67 us  [exchange(): return lax.all_to_all(chunks, axis, 0, 0)]
    all_to_all x10 -> x9, waiting for transfers between devices: 128 us -> 131 us  [exchange(): return lax.all_to_all(chunks, axis, 0, 0)]
    unnamed x37 -> x15, local copies, waits for them, and re-layouts: 6.87 us -> 7.59 us
  transfers between devices with their start and end apart: 10 -> 9, of which waited for: 10 -> 9; matrix products, arithmetic and copies ran while one was open for 8% -> 4% of each run, Pallas kernels for 0% -> 2%
where the time goes in v1:
time: 307 us; the launch traced here: 306 us
  waiting for transfers between devices  131 us (43%)
  starting transfers between devices  67 us (22%)
  Pallas kernels  41.9 us (14%)
  blocking collectives  34 us (11%)
  local copies, waits for them, and re-layouts  16.2 us (5%)
  matrix products  11.8 us (4%)
    all_to_all x9, waiting for transfers between devices, exchange(): return lax.all_to_all(chunks, axis, 0, 0)  131 us
    all_to_all x9, starting transfers between devices, exchange(): return lax.all_to_all(chunks, axis, 0, 0)  67 us
    pallas_call x5, Pallas kernels, launch(): pl.pallas_call(kernel, out_shape=outs, in_specs=[pl.BlockSpec(memory_spac...  41.9 us
    all_to_all x2, blocking collectives, exchange(): return lax.all_to_all(chunks, axis, 0, 0)  34 us
    dot_general x29, matrix products, dot(): lax.dot_general(left_side, right_side, (((left_dim,), (right_dim,)), ((),...  11.8 us
    unnamed x15, local copies, waits for them, and re-layouts  7.59 us
  transfers between devices with their start and end apart: 9, of which 9 were waited for; matrix products, arithmetic and copies ran while one was open for 4% of the time, Pallas kernels for 2%

profile of v1, /device:TPU:1, one launch (start us, length us, event | category | flops | bytes accessed | tf_op | source)
XLA Modules:
  0.0 305.6 jit_solution(5464534058729932882)
XLA Ops:
  0.1 1.8 copy.12
  1.9 1.3 fusion
  3.4 22.5 %all_to_all.55 = f32[32,40,128]{2,1,0:T(8,128)S(1)} all-to-all(f32[32,40,128]{2,1,0:T(8,128)S(1)} %pad_maximum_fusion.2), channel_id=1, replica_groups=mesh['row'=16,'col'=32] {'col'}, dimensions={0} | all-to-all | bytes 1310720 | tf_op jit(solution)/shard_map/all_to_all | solution.py:52
  25.9 0.9 broadcast_in_dim.48
  26.8 13.7 %all-to-all-start.1 = ((f32[16,72,128]{2,1,0:T(8,128)}), f32[16,72,128]{2,1,0:T(8,128)S(1)}, u32[]{:S(2)}, u32[]{:S(2)}) async-start(f32[16,72,128]{2,1,0:T(8,128)} %broadcast_in_dim.48), calls=%async_computation.1 | async-start | bytes 1179648 | tf_op jit(solution)/shard_map/all_to_all | solution.py:52
  40.5 0.9 broadcast_dynamic-update-slice_fusion.1
  41.4 26.3 %all-to-all-done.1 = f32[16,72,128]{2,1,0:T(8,128)S(1)} async-done(((f32[16,72,128]{2,1,0:T(8,128)}), f32[16,72,128]{2,1,0:T(8,128)S(1)}, u32[]{:S(2)}, u32[]{:S(2)}) %all-to-all-start.1) | async-done | bytes 589856 | tf_op jit(solution)/shard_map/all_to_all | solution.py:52
  67.8 0.7 constant_dynamic-update-slice_fusion.1
  68.6 0.9 broadcast_dynamic-update-slice_fusion
  69.5 0.7 constant_dynamic-update-slice_fusion
  70.3 0.7 broadcast_dynamic-update-slice_fusion.2
  70.9 9.8 %all-to-all-start.2 = ((f32[32,104,128]{2,1,0:T(8,128)}), f32[32,104,128]{2,1,0:T(8,128)S(1)}, u32[]{:S(2)}, u32[]{:S(2)}) async-start(f32[32,104,128]{2,1,0:T(8,128)} %broadcast_dynamic-update-slice_fusion.2), calls=%async_computation.2 | async-start | bytes 3407872 | tf_op jit(solution)/shard_map/all_to_all | solution.py:52
  80.8 0.6 pad_add_fusion.refs_0_
  81.4 23.6 %all-to-all-done.2.refs_5_.refs_10_ = f32[32,104,128]{2,1,0:T(8,128)S(1)} async-done(((f32[32,104,128]{2,1,0:T(8,128)}), f32[32,104,128]{2,1,0:T(8,128)S(1)}, u32[]{:S(2)}, u32[]{:S(2)}) %all-to-all-start.2) | async-done | bytes 1703968 | tf_op jit(solution)/shard_map/all_to_all | solution.py:52
  105.0 0.7 slice_bitcast_fusion.refs_1_
  105.7 0.9 fusion.8
  106.6 11.7 %shard_map.17 = (f32[32,40,128]{2,1,0:T(8,128)}, f32[512,128]{1,0:T(8,128)}, f32[512,128]{1,0:T(8,128)}, f32[512,128]{1,0:T(8,128)}, f32[128,128]{1,0:T(8,128)}) custom-call(s32[2]{0:T(128)} %pad_add_fusion.refs_0_, f32[256,128]{1,0:T(8,128)} %slice_bitcast_fusion.refs_1_, f32[512,128]{1,0:T(8,128)} %bitcast.109, f32[512,128]{1,0:T(8,128)} %bitcast.108, ...), custom_call_target="tpu_custom_call" | custom-call | tf_op jit(solution)/shard_map/pallas_call | solution.py:114
  118.3 4.2 %all-to-all-start.3 = ((f32[32,40,128]{2,1,0:T(8,128)}), f32[32,40,128]{2,1,0:T(8,128)S(1)}, u32[]{:S(2)}, u32[]{:S(2)}) async-start(f32[32,40,128]{2,1,0:T(8,128)} %get-tuple-element.22), calls=%async_computation.3 | async-start | bytes 1310720 | tf_op jit(solution)/shard_map/all_to_all | solution.py:52
  122.6 1.1 fusion.4
  123.9 1.0 convolution_add_fusion.13
  125.2 10.4 %all-to-all-done.3 = f32[32,40,128]{2,1,0:T(8,128)S(1)} async-done(((f32[32,40,128]{2,1,0:T(8,128)}), f32[32,40,128]{2,1,0:T(8,128)S(1)}, u32[]{:S(2)}, u32[]{:S(2)}) %all-to-all-start.3) | async-done | bytes 655392 | tf_op jit(solution)/shard_map/all_to_all | solution.py:52
  135.6 0.7 broadcast_in_dim.52
  136.4 5.4 %all-to-all-start.4 = ((f32[16,40,128]{2,1,0:T(8,128)}), f32[16,40,128]{2,1,0:T(8,128)S(1)}, u32[]{:S(2)}, u32[]{:S(2)}) async-start(f32[16,40,128]{2,1,0:T(8,128)} %broadcast_in_dim.52), calls=%async_computation.4 | async-start | bytes 655360 | tf_op jit(solution)/shard_map/all_to_all | solution.py:52
  141.8 0.2 convolution_add_fusion.12
  142.3 0.2 convolution_add_fusion.11
  142.7 0.2 convolution_add_fusion.10
  142.9 0.2 fusion.14
  143.1 15.7 %all-to-all-done.4 = f32[16,40,128]{2,1,0:T(8,128)S(1)} async-done(((f32[16,40,128]{2,1,0:T(8,128)}), f32[16,40,128]{2,1,0:T(8,128)S(1)}, u32[]{:S(2)}, u32[]{:S(2)}) %all-to-all-start.4) | async-done | bytes 327712 | tf_op jit(solution)/shard_map/all_to_all | solution.py:52
  159.0 1.0 pad_maximum_fusion
  160.0 8.9 %all-to-all-start.5 = ((f32[32,56,128]{2,1,0:T(8,128)}), f32[32,56,128]{2,1,0:T(8,128)S(1)}, u32[]{:S(2)}, u32[]{:S(2)}) async-start(f32[32,56,128]{2,1,0:T(8,128)} %pad_maximum_fusion), calls=%async_computation.5 | async-start | bytes 1835008 | tf_op jit(solution)/shard_map/all_to_all | solution.py:52
  168.9 0.2 convolution_add_fusion.9
  169.3 0.2 convolution_add_fusion.8
  169.6 0.8 convolution_add_fusion.7.refs_2_.refs_3_
  170.4 14.2 %all-to-all-done.5.refs_1_.refs_2_ = f32[32,56,128]{2,1,0:T(8,128)S(1)} async-done(((f32[32,56,128]{2,1,0:T(8,128)}), f32[32,56,128]{2,1,0:T(8,128)S(1)}, u32[]{:S(2)}, u32[]{:S(2)}) %all-to-all-start.5) | async-done | bytes 917536 | tf_op jit(solution)/shard_map/all_to_all | solution.py:52
  184.6 0.9 copy-done.2
  185.5 5.2 %shard_map.18 = (f32[32,8,128]{2,1,0:T(8,128)}, f32[128,128]{1,0:T(8,128)}, f32[128,128]{1,0:T(8,128)}, f32[512,128]{1,0:T(8,128)}) custom-call(s32[2]{0:T(128)} %pad_add_fusion.refs_0_, f32[32,56,128]{2,1,0:T(8,128)} %copy-done.2, f32[128,128]{1,0:T(8,128)} %convolution_add_fusion.7.refs_2_.refs_3_, f32[512,128]{1,0:T(8,128)} %get-tuple-element.24.refs_3_.refs_7_, ...), custom_call_target="tpu_custom_call" | custom-call | tf_op jit(solution)/shard_map/pallas_call | solution.py:114
  190.7 11.5 %all_to_all.56 = f32[32,8,128]{2,1,0:T(8,128)S(1)} all-to-all(f32[32,8,128]{2,1,0:T(8,128)} %get-tuple-element.30), channel_id=1, replica_groups=mesh['row'=16,'col'=32] {'col'}, dimensions={0} | all-to-all | bytes 262144 | tf_op jit(solution)/shard_map/all_to_all | solution.py:52
  202.2 0.7 broadcast_in_dim.97
  202.9 3.9 %all-to-all-start.7 = ((f32[32,8,128]{2,1,0:T(8,128)}), f32[32,8,128]{2,1,0:T(8,128)S(1)}, u32[]{:S(2)}, u32[]{:S(2)}) async-start(f32[32,8,128]{2,1,0:T(8,128)} %broadcast_in_dim.97), calls=%async_computation.7 | async-start | bytes 262144 | tf_op jit(solution)/shard_map/all_to_all | solution.py:52
  206.8 7.1 %shard_map.19 = (f32[1024,512]{1,0:T(8,128)}, f32[512,128]{1,0:T(8,128)}, f32[512,128]{1,0:T(8,128)}) custom-call(s32[2]{0:T(128)} %pad_add_fusion.refs_0_, f32[1024,512]{1,0:T(8,128)} %bitcast.100, f32[32,56,128]{2,1,0:T(8,128)} %copy-done.2, f32[128,128]{1,0:T(8,128)} %convolution_add_fusion.7.refs_2_.refs_3_, f32[128,128]{1,0:T(8,128)} %get-tuple-element.25.refs_4_, ...), custom_call_target="tpu_custom_call" | custom-call | tf_op jit(solution)/shard_map/pallas_call | solution.py:114
  213.9 0.7 all-to-all-done.7
  214.6 0.7 copy-done.4
  215.3 11.7 %shard_map.20 = (f32[32,40,128]{2,1,0:T(8,128)}, f32[512,128]{1,0:T(8,128)}, f32[512,128]{1,0:T(8,128)}, f32[512,128]{1,0:T(8,128)}, f32[128,128]{1,0:T(8,128)}) custom-call(s32[2]{0:T(128)} %pad_add_fusion.refs_0_, f32[256,128]{1,0:T(8,128)} %bitcast.115, f32[512,128]{1,0:T(8,128)} %get-tuple-element.31.refs_2_, f32[512,128]{1,0:T(8,128)} %get-tuple-element.32.refs_3_, ...), custom_call_target="tpu_custom_call" | custom-call | tf_op jit(solution)/shard_map/pallas_call | solution.py:114
  227.0 6.8 %all-to-all-start.8 = ((f32[32,40,128]{2,1,0:T(8,128)}), f32[32,40,128]{2,1,0:T(8,128)S(1)}, u32[]{:S(2)}, u32[]{:S(2)}) async-start(f32[32,40,128]{2,1,0:T(8,128)} %get-tuple-element.34), calls=%async_computation.8 | async-start | bytes 1310720 | tf_op jit(solution)/shard_map/all_to_all | solution.py:52
  233.8 1.1 fusion.5
  234.9 1.0 convolution_add_fusion.6
  236.4 10.3 %all-to-all-done.8 = f32[32,40,128]{2,1,0:T(8,128)S(1)} async-done(((f32[32,40,128]{2,1,0:T(8,128)}), f32[32,40,128]{2,1,0:T(8,128)S(1)}, u32[]{:S(2)}, u32[]{:S(2)}) %all-to-all-start.8) | async-done | bytes 655392 | tf_op jit(solution)/shard_map/all_to_all | solution.py:52
  246.8 0.7 broadcast_in_dim.99
  247.5 5.4 %all-to-all-start.9 = ((f32[16,40,128]{2,1,0:T(8,128)}), f32[16,40,128]{2,1,0:T(8,128)S(1)}, u32[]{:S(2)}, u32[]{:S(2)}) async-start(f32[16,40,128]{2,1,0:T(8,128)} %broadcast_in_dim.99), calls=%async_computation.9 | async-start | bytes 655360 | tf_op jit(solution)/shard_map/all_to_all | solution.py:52
  253.0 0.2 convolution_add_fusion.5
  253.2 0.2 fusion.18
  253.4 0.2 convolution_add_fusion.4
  253.8 0.2 convolution_add_fusion.3
  254.3 15.8 %all-to-all-done.9 = f32[16,40,128]{2,1,0:T(8,128)S(1)} async-done(((f32[16,40,128]{2,1,0:T(8,128)}), f32[16,40,128]{2,1,0:T(8,128)S(1)}, u32[]{:S(2)}, u32[]{:S(2)}) %all-to-all-start.9) | async-done | bytes 327712 | tf_op jit(solution)/shard_map/all_to_all | solution.py:52
  270.2 1.0 pad_maximum_fusion.1
  271.2 8.7 %all-to-all-start.10 = ((f32[32,56,128]{2,1,0:T(8,128)}), f32[32,56,128]{2,1,0:T(8,128)S(1)}, u32[]{:S(2)}, u32[]{:S(2)}) async-start(f32[32,56,128]{2,1,0:T(8,128)} %pad_maximum_fusion.1), calls=%async_computation.10 | async-start | bytes 1835008 | tf_op jit(solution)/shard_map/all_to_all | solution.py:52
  279.9 0.2 convolution_add_fusion.2
  280.1 0.2 fusion.21
  280.3 0.2 convolution_add_fusion.1
  280.5 0.8 convolution_add_fusion.refs_3_
  281.4 14.2 %all-to-all-done.10.refs_2_ = f32[32,56,128]{2,1,0:T(8,128)S(1)} async-done(((f32[32,56,128]{2,1,0:T(8,128)}), f32[32,56,128]{2,1,0:T(8,128)S(1)}, u32[]{:S(2)}, u32[]{:S(2)}) %all-to-all-start.10) | async-done | bytes 917536 | tf_op jit(solution)/shard_map/all_to_all | solution.py:52
  295.6 0.9 copy-done.3
  296.5 6.2 %shard_map.21 = f32[1024,512]{1,0:T(8,128)} custom-call(s32[2]{0:T(128)} %pad_add_fusion.refs_0_, f32[1024,512]{1,0:T(8,128)} %get-tuple-element.29.refs_5_.refs_1_, f32[32,56,128]{2,1,0:T(8,128)} %copy-done.3, f32[128,128]{1,0:T(8,128)} %convolution_add_fusion.refs_3_, f32[512,128]{1,0:T(8,128)} %get-tuple-element.36.refs_4_, ...), custom_call_target="tpu_custom_call" | custom-call | tf_op jit(solution)/shard_map/pallas_call | solution.py:114
  302.7 2.9 reshape.89
  (45 shorter events, 2.6 us)
Async XLA Ops:
  1.9 1.6 copy-start
  26.8 40.9 %all-to-all-start.1 = ((f32[16,72,128]{2,1,0:T(8,128)}), f32[16,72,128]{2,1,0:T(8,128)S(1)}, u32[]{:S(2)}, u32[]{:S(2)}) async-start(f32[16,72,128]{2,1,0:T(8,128)} %broadcast_in_dim.48), calls=%async_computation.1 | async-start | bytes 1179648 | tf_op jit(solution)/shard_map/all_to_all | solution.py:52
  70.9 34.1 %all-to-all-start.2 = ((f32[32,104,128]{2,1,0:T(8,128)}), f32[32,104,128]{2,1,0:T(8,128)S(1)}, u32[]{:S(2)}, u32[]{:S(2)}) async-start(f32[32,104,128]{2,1,0:T(8,128)} %broadcast_dynamic-update-slice_fusion.2), calls=%async_computation.2 | async-start | bytes 3407872 | tf_op jit(solution)/shard_map/all_to_all | solution.py:52
  105.0 13.3 %copy-start.1 = (f32[32,104,128]{2,1,0:T(8,128)}, f32[32,104,128]{2,1,0:T(8,128)S(1)}, u32[]{:S(2)}) copy-start(f32[32,104,128]{2,1,0:T(8,128)S(1)} %all-to-all-done.2.refs_5_.refs_10_) | copy-start | bytes 5111812
  118.3 17.3 %all-to-all-start.3 = ((f32[32,40,128]{2,1,0:T(8,128)}), f32[32,40,128]{2,1,0:T(8,128)S(1)}, u32[]{:S(2)}, u32[]{:S(2)}) async-start(f32[32,40,128]{2,1,0:T(8,128)} %get-tuple-element.22), calls=%async_computation.3 | async-start | bytes 1310720 | tf_op jit(solution)/shard_map/all_to_all | solution.py:52
  136.4 22.5 %all-to-all-start.4 = ((f32[16,40,128]{2,1,0:T(8,128)}), f32[16,40,128]{2,1,0:T(8,128)S(1)}, u32[]{:S(2)}, u32[]{:S(2)}) async-start(f32[16,40,128]{2,1,0:T(8,128)} %broadcast_in_dim.52), calls=%async_computation.4 | async-start | bytes 655360 | tf_op jit(solution)/shard_map/all_to_all | solution.py:52
  160.0 24.6 %all-to-all-start.5 = ((f32[32,56,128]{2,1,0:T(8,128)}), f32[32,56,128]{2,1,0:T(8,128)S(1)}, u32[]{:S(2)}, u32[]{:S(2)}) async-start(f32[32,56,128]{2,1,0:T(8,128)} %pad_maximum_fusion), calls=%async_computation.5 | async-start | bytes 1835008 | tf_op jit(solution)/shard_map/all_to_all | solution.py:52
  184.6 0.9 copy-start.2
  202.9 11.7 %all-to-all-start.7 = ((f32[32,8,128]{2,1,0:T(8,128)}), f32[32,8,128]{2,1,0:T(8,128)S(1)}, u32[]{:S(2)}, u32[]{:S(2)}) async-start(f32[32,8,128]{2,1,0:T(8,128)} %broadcast_in_dim.97), calls=%async_computation.7 | async-start | bytes 262144 | tf_op jit(solution)/shard_map/all_to_all | solution.py:52
  214.6 0.7 copy-start.4
  227.0 19.7 %all-to-all-start.8 = ((f32[32,40,128]{2,1,0:T(8,128)}), f32[32,40,128]{2,1,0:T(8,128)S(1)}, u32[]{:S(2)}, u32[]{:S(2)}) async-start(f32[32,40,128]{2,1,0:T(8,128)} %get-tuple-element.34), calls=%async_computation.8 | async-start | bytes 1310720 | tf_op jit(solution)/shard_map/all_to_all | solution.py:52
  247.5 22.5 %all-to-all-start.9 = ((f32[16,40,128]{2,1,0:T(8,128)}), f32[16,40,128]{2,1,0:T(8,128)S(1)}, u32[]{:S(2)}, u32[]{:S(2)}) async-start(f32[16,40,128]{2,1,0:T(8,128)} %broadcast_in_dim.99), calls=%async_computation.9 | async-start | bytes 655360 | tf_op jit(solution)/shard_map/all_to_all | solution.py:52
  271.2 24.4 %all-to-all-start.10 = ((f32[32,56,128]{2,1,0:T(8,128)}), f32[32,56,128]{2,1,0:T(8,128)S(1)}, u32[]{:S(2)}, u32[]{:S(2)}) async-start(f32[32,56,128]{2,1,0:T(8,128)} %pad_maximum_fusion.1), calls=%async_computation.10 | async-start | bytes 1835008 | tf_op jit(solution)/shard_map/all_to_all | solution.py:52
  295.5 0.9 copy-start.3

commit v2 on v1

--- a/solution.py
+++ b/solution.py
@@ -38,14 +38,15 @@
     return product(left_high, right_high) + (product(left_high, right_low) + product(left_low, right_high))
 
 
-def newton_inverse(middle):
-    identity = jnp.eye(middle.shape[0], dtype=jnp.float32)
+def newton_body(place, middle):
+    identity = eye_of(middle.shape[0])
     power = identity - middle
+
     approx = identity + power
     for sweep_step in range(1, newton_sweeps):
         power = dot(power, power)
         approx = approx + dot(approx, power)
-    return approx
+    return (approx,)
 
 
 def exchange(chunks, axis):
@@ -100,7 +101,7 @@
     return scratch[...]
 
 
-def launch(body, shapes, place, *operands, scratch=None):
+def launch(body, shapes, place, *operands, scratch=None, lines=None):
     outs = [jax.ShapeDtypeStruct(shape, jnp.float32) for shape in shapes]
 
     def kernel(*refs):
@@ -108,7 +109,12 @@
         inputs = refs[1 : 1 + len(operands)]
         results = body(refs[0], *[ref[...] for ref in inputs], *extra)
         for ref, value in zip(refs[1 + len(operands) : 1 + len(operands) + len(outs)], results, strict=True):
-            ref[...] = value
+            if lines:
+                width = value.shape[1] // lines
+                for u in range(lines):
+                    ref[pl.ds(u, value.shape[0], stride=lines), :] = value[:, u * width : (u + 1) * width]
+            else:
+                ref[...] = value
 
     vmem = pl.BlockSpec(memory_space=pltpu.VMEM)
     return pl.pallas_call(
@@ -138,6 +144,8 @@
         q = dot(keep_from(panel, block, index, first), lower_inverse, 1, 1)
         return first_tile(q, block, lambda tile: tile + identity * jnp.where(index == first, 1.0, 0.0))
 
+    if panel_cols.shape[0] == block:
+        panel_cols = panel_cols.T
     cols = reflect(panel_cols, place[1])
     even = reflect(panel_even, place[0])
     odd = dot(panel_odd, lower_inverse, 1, 1)
@@ -168,15 +176,14 @@
     return [dot(w, inverse_core, 1, 1) - 0.5 * dot(v, core_block) for w, v in pairs]
 
 
-def middle_body(place, got, inverse_core, cols, pivot_tile, shared, *, first, sizes):
+def middle_body(place, got, inverse_core, cols, pivot_tile, next_tile, *, first, sizes):
     block, spread, part, col_count, small, tile_cols = sizes
     little = got[:, (spread + 1) * part :].reshape(col_count * small, block)
     core_block = dot(dot(inverse_core, little[:block]), inverse_core, 1, 1)
     w_cols = split_shared(got, 0, sizes)[1]
     companion = dot(w_cols, inverse_core, 1, 1) - 0.5 * dot(cols, core_block)
     companion_tile = dot(little[block:], inverse_core, 1, 1) - 0.5 * dot(pivot_tile, core_block)
-    panel = split_shared(shared, (spread + 1) * part, sizes)[1]
-    panel = panel - (dot(cols, companion_tile, 1, 1) + dot(companion, pivot_tile, 1, 1))
+    panel = next_tile.T - (dot(cols, companion_tile, 1, 1) + dot(companion, pivot_tile, 1, 1))
     masked = keep_from(panel, block, place[1], first + 1)
     gram = dot(masked.T, masked)
     top = panel[:block] * jnp.where(place[1] == first + 1, 1.0, 0.0)
@@ -195,7 +202,9 @@
 def between_body(place, current, got, inverse_core, core_block, even, odd, cols, companion_tile, pivot_tile, shared, *, sizes):
     block, spread, part, col_count, small, tile_cols = sizes
     even_z, odd_z, cols_z = companions(got, inverse_core, even, odd, cols, core_block, sizes)
-    (next_even, next_odd), unused = split_shared(shared, (spread + 1) * part, sizes)
+    next_even, next_odd = (
+        shared[:, part * h : part * h + part].reshape(col_count * part, block) for h in range(spread)
+    )
     panels = [
         values - (dot(v, companion_tile, 1, 1) + dot(z, pivot_tile, 1, 1))
         for values, v, z in ((next_even, even, even_z), (next_odd, odd, odd_z))
@@ -229,17 +238,27 @@
         split = values.reshape(tile_cols, spread, block // part, part, block)
         return split.transpose(0, 2, 1, 3, 4).reshape(col_count, chunk, block)
 
-    def share(mine, count):
-        got = exchange(jnp.broadcast_to(mine[None], (row_count,) + mine.shape), "row")
-        sends = []
-        for index in range(count):
-            piece = mine[index * chunk : (index + 1) * chunk]
-            sends.append(jnp.broadcast_to(piece[None], (col_count, chunk, block)))
-            wanted = got[:, index * chunk : (index + 1) * chunk].reshape(row_count, spread, part, block)
-            sends.append(wanted.transpose(1, 0, 2, 3).reshape(col_count, part, block))
-        total = got[:, count * chunk :].sum(0)
-        sends.append(jnp.broadcast_to(total[None], (col_count,) + total.shape))
+    def copies_of(value, count):
+        return jnp.broadcast_to(value[None], (count,) + value.shape)
+
+    def share(mine, got):
+        wanted = got[:, :chunk].reshape(row_count, spread, part, block)
+        wanted = wanted.transpose(1, 0, 2, 3).reshape(col_count, part, block)
+        total = got[:, chunk:].sum(0)
+        sends = [copies_of(mine[:chunk], col_count), wanted, copies_of(total, col_count)]
         return exchange(jnp.concatenate(sends, axis=1), "col")
+
+    def only_at(value, source):
+        return jnp.where(row_index == source, value, 0.0)
+
+    def hop(held, source, step):
+        if step >= row_count:
+            return held
+        pairs = [((source + k) % row_count, (source + k + step) % row_count) for k in range(0, row_count, 2 * step)]
+        return held + lax.ppermute(held, "row", pairs)
+
+    def after(value, held):
+        return lax.optimization_barrier((value, held))
 
     current = matrix.reshape(rows, cols)
 
@@ -250,10 +269,16 @@
     top_part = jnp.where(row_index == 1, own_col[:block], 0.0)
     stacked = jnp.concatenate([gram_part, top_part]).reshape(col_count, small, block)
     got = exchange(jnp.concatenate([chunks_of(own_col), stacked], axis=1), "col")
-    shared = share(jnp.concatenate([got[0, :chunk], got[1, :chunk], got[0, chunk:]]), 2)
-    stacked = shared[:, 2 * (chunk + part) :].reshape(2 * block, block)
+    got, panel_cols = after(got, hop(only_at(current[:block], 0), 0, 8))
+    next_chunk = got[1, :chunk]
+    total = exchange(copies_of(got[0, chunk:], row_count), "row")
+    total, panel_cols = after(total, hop(panel_cols, 0, 4))
+    total = total.sum(0)
+    shared = exchange(copies_of(jnp.concatenate([got[0, :chunk], total]), col_count), "col")
+    panel_cols = hop(hop(panel_cols, 0, 2), 0, 1)
+    shared, next_tile = after(shared, only_at(current[:block], 1))
+    stacked = shared[:, chunk:].reshape(2 * block, block)
     even, odd = (shared[:, part * h : part * h + part].reshape(cols, block) for h in range(spread))
-    panel_cols = shared[:, chunk : chunk + part].reshape(cols, block)
 
     for panel_index in range(2):
         last = panel_index == 1
@@ -263,23 +288,31 @@
             [(col_count, chunk + small, block), tall, tall, tall, tile],
             place, stacked, even, odd, panel_cols, current, scratch=tile,
         )
-        inverse_core = newton_inverse(pivot_tile)
-        got = share(exchange(send, "col").sum(0), 1)
+        (inverse_core,) = launch(newton_body, [tile], place, pivot_tile)
+        if last:
+            mine = exchange(send, "col").sum(0)
+            got = share(mine, exchange(copies_of(mine, row_count), "row"))
+        else:
+            send, next_tile = after(send, hop(next_tile, 1, 8))
+            mine, next_tile = after(exchange(send, "col"), hop(next_tile, 1, 4))
+            mine = mine.sum(0)
+            rest, next_tile = after(exchange(copies_of(mine, row_count), "row"), hop(next_tile, 1, 2))
+            got, next_tile = after(share(mine, rest), hop(next_tile, 1, 1))
         if last:
             (current,) = launch(
                 functools.partial(final_body, sizes=sizes),
-                [(rows, cols)],
-                place, current, got, inverse_core, even, odd, panel_cols,
+                [(rows * tile_cols, block)],
+                place, current, got, inverse_core, even, odd, panel_cols, lines=tile_cols,
             )
             break
         send, core_block, companion_tile, next_cols = launch(
             functools.partial(middle_body, first=first, sizes=sizes),
             [(col_count, small, block), tile, tile, tall],
-            place, got, inverse_core, panel_cols, pivot_tile, shared,
+            place, got, inverse_core, panel_cols, pivot_tile, next_tile,
         )
-        total = exchange(send, "col").sum(0)
-        copies = jnp.broadcast_to(total[None], (col_count, small, block))
-        stacked = exchange(copies, "col").reshape(2 * block, block)
+        shared = exchange(jnp.concatenate([copies_of(next_chunk, col_count), send], axis=1), "col")
+        total = shared[:, chunk:].sum(0)
+        stacked = exchange(copies_of(total, col_count), "col").reshape(2 * block, block)
         current, even, odd = launch(
             functools.partial(between_body, sizes=sizes),
             [(rows, cols), tall, tall],

time: 307 us -> 307 us (level)
  starting transfers between devices: 67 us -> 107 us
  waiting for transfers between devices: 131 us -> 94.8 us
  matrix products: 11.8 us -> 1.31 us
  local copies, waits for them, and re-layouts: 16.2 us -> 10.1 us
  other arithmetic: 2.85 us -> 8.8 us
  Pallas kernels: 41.9 us -> 47.8 us
    all_to_all x9, waiting for transfers between devices: 131 us -> 73.8 us  [exchange(): return lax.all_to_all(chunks, axis, 0, 0)]
    ppermute x0 -> x8, starting transfers between devices: none -> 22.3 us  [hop(): return held + lax.ppermute(held, 'row', pairs)]
    ppermute x0 -> x8, waiting for transfers between devices: none -> 21 us  [hop(): return held + lax.ppermute(held, 'row', pairs)]
    all_to_all x9, starting transfers between devices: 67 us -> 84.3 us  [exchange(): return lax.all_to_all(chunks, axis, 0, 0)]
    dot_general x29 -> x1, matrix products: 11.8 us -> 1.31 us  [dot(): lax.dot_general(left_side, right_side, (((left_dim,), (right_dim,)), ((),...]
    pallas_call x5 -> x7, Pallas kernels: 41.9 us -> 47.8 us  [launch(): pl.pallas_call(kernel, out_shape=outs, in_specs=[pl.BlockSpec(memory_spac...]
    unnamed x15 -> x13, local copies, waits for them, and re-layouts: 7.59 us -> 4.38 us
  transfers between devices with their start and end apart: 9 -> 17, of which waited for: 9 -> 11; matrix products, arithmetic and copies ran while one was open for 4% -> 2% of each run, Pallas kernels for 2% -> 8%
where the time goes in v2:
time: 307 us; the launch traced here: 306 us
  starting transfers between devices  107 us (35%)
  waiting for transfers between devices  94.8 us (31%)
  Pallas kernels  47.8 us (16%)
  blocking collectives  36.1 us (12%)
  local copies, waits for them, and re-layouts  10.1 us (3%)
  other arithmetic  8.8 us (3%)
    all_to_all x9, starting transfers between devices, exchange(): return lax.all_to_all(chunks, axis, 0, 0)  84.3 us
    all_to_all x9, waiting for transfers between devices, exchange(): return lax.all_to_all(chunks, axis, 0, 0)  73.8 us
    pallas_call x7, Pallas kernels, launch(): pl.pallas_call(kernel, out_shape=outs, in_specs=[pl.BlockSpec(memory_spac...  47.8 us
    all_to_all x2, blocking collectives, exchange(): return lax.all_to_all(chunks, axis, 0, 0)  36.1 us
    ppermute x8, starting transfers between devices, hop(): return held + lax.ppermute(held, 'row', pairs)  22.3 us
    ppermute x8, waiting for transfers between devices, hop(): return held + lax.ppermute(held, 'row', pairs)  21 us
  transfers between devices with their start and end apart: 17, of which 11 were waited for; matrix products, arithmetic and copies ran while one was open for 2% of the time, Pallas kernels for 8%

profile of v2, /device:TPU:1, one launch (start us, length us, event | category | flops | bytes accessed | tf_op | source)
XLA Modules:
  0.0 306.0 jit_solution(9850966975732888863)
XLA Ops:
  0.0 0.1 broadcast_bitcast_fusion
  0.1 1.8 copy.16
  1.9 0.1 slice.67
  1.9 1.3 fusion
  3.3 0.1 copy.4
  3.3 0.9 pad_maximum_fusion.2
  4.2 10.4 %all-to-all-start = ((f32[32,40,128]{2,1,0:T(8,128)}), f32[32,40,128]{2,1,0:T(8,128)S(1)}, u32[]{:S(2)}, u32[]{:S(2)}) async-start(f32[32,40,128]{2,1,0:T(8,128)} %pad_maximum_fusion.2), calls=%async_computation | async-start | bytes 1310720 | tf_op jit(solution)/shard_map/all_to_all | solution.py:53
  14.6 2.4 fusion.3
  17.1 13.6 %collective-permute-start = (f32[128,512]{1,0:T(8,128)S(1)}, f32[128,512]{1,0:T(8,128)S(1)}, u32[]{:S(2)}, u32[]{:S(2)}) collective-permute-start(f32[128,512]{1,0:T(8,128)S(1)} %bitcast.69), channel_id=1, source_target_pairs={{0,256},{1,257},{2,258},{3,259},{4,260},{5,261},{6,262},{7,263},{8... | collective-permute-start | bytes 786440 | tf_op jit(solution)/shard_map/ppermute | solution.py:258
  30.8 5.4 %collective-permute-done = f32[128,512]{1,0:T(8,128)S(1)} collective-permute-done((f32[128,512]{1,0:T(8,128)S(1)}, f32[128,512]{1,0:T(8,128)S(1)}, u32[]{:S(2)}, u32[]{:S(2)}) %collective-permute-start) | collective-permute-done | bytes 262176 | tf_op jit(solution)/shard_map/ppermute | solution.py:258
  36.2 1.3 collective-permute-start.1
  37.5 0.6 broadcast_in_dim.92
  38.2 12.3 %all-to-all-start.1 = ((f32[16,8,128]{2,1,0:T(8,128)}), f32[16,8,128]{2,1,0:T(8,128)S(1)}, u32[]{:S(2)}, u32[]{:S(2)}) async-start(f32[16,8,128]{2,1,0:T(8,128)} %broadcast_in_dim.92), calls=%async_computation.1 | async-start | bytes 131072 | tf_op jit(solution)/shard_map/all_to_all | solution.py:53
  50.5 11.5 %all-to-all-done.1 = f32[16,8,128]{2,1,0:T(8,128)S(1)} async-done(((f32[16,8,128]{2,1,0:T(8,128)}), f32[16,8,128]{2,1,0:T(8,128)S(1)}, u32[]{:S(2)}, u32[]{:S(2)}) %all-to-all-start.1) | async-done | bytes 65568 | tf_op jit(solution)/shard_map/all_to_all | solution.py:53
  62.1 0.9 broadcast_in_dim.93
  63.0 9.6 %all-to-all-start.2 = ((f32[32,40,128]{2,1,0:T(8,128)}), f32[32,40,128]{2,1,0:T(8,128)S(1)}, u32[]{:S(2)}, u32[]{:S(2)}) async-start(f32[32,40,128]{2,1,0:T(8,128)} %broadcast_in_dim.93), calls=%async_computation.2 | async-start | bytes 1310720 | tf_op jit(solution)/shard_map/all_to_all | solution.py:53
  72.6 2.8 collective-permute-start.2
  75.4 5.4 %collective-permute-done.2 = f32[128,512]{1,0:T(8,128)S(1)} collective-permute-done((f32[128,512]{1,0:T(8,128)S(1)}, f32[128,512]{1,0:T(8,128)S(1)}, u32[]{:S(2)}, u32[]{:S(2)}) %collective-permute-start.2) | collective-permute-done | bytes 262176 | tf_op jit(solution)/shard_map/ppermute | solution.py:258
  80.9 1.3 collective-permute-start.3
  82.2 0.6 pad_add_fusion.refs_0_
  82.8 4.2 %collective-permute-done.3 = f32[128,512]{1,0:T(8,128)S(1)} collective-permute-done((f32[128,512]{1,0:T(8,128)S(1)}, f32[128,512]{1,0:T(8,128)S(1)}, u32[]{:S(2)}, u32[]{:S(2)}) %collective-permute-start.3) | collective-permute-done | bytes 262176 | tf_op jit(solution)/shard_map/ppermute | solution.py:258
  87.0 0.7 add.35.refs_4_
  87.7 0.7 collective-permute-start.4
  88.4 0.7 slice_bitcast_fusion.refs_1_
  89.1 0.8 fusion.9
  89.9 11.7 %shard_map.17 = (f32[32,40,128]{2,1,0:T(8,128)}, f32[512,128]{1,0:T(8,128)}, f32[512,128]{1,0:T(8,128)}, f32[512,128]{1,0:T(8,128)}, f32[128,128]{1,0:T(8,128)}) custom-call(s32[2]{0:T(128)} %pad_add_fusion.refs_0_, f32[256,128]{1,0:T(8,128)} %slice_bitcast_fusion.refs_1_, f32[512,128]{1,0:T(8,128)} %bitcast.65, f32[512,128]{1,0:T(8,128)} %bitcast.64, ...), custom_call_target="tpu_custom_call" | custom-call | tf_op jit(solution)/shard_map/pallas_call | solution.py:120
  101.7 8.5 %all-to-all-start.3 = ((f32[32,40,128]{2,1,0:T(8,128)}), f32[32,40,128]{2,1,0:T(8,128)S(1)}, u32[]{:S(2)}, u32[]{:S(2)}) async-start(f32[32,40,128]{2,1,0:T(8,128)} %get-tuple-element.43), calls=%async_computation.3 | async-start | bytes 1310720 | tf_op jit(solution)/shard_map/all_to_all | solution.py:53
  110.2 0.7 collective-permute-start.5
  111.0 12.2 %all-to-all-done.3 = f32[32,40,128]{2,1,0:T(8,128)S(1)} async-done(((f32[32,40,128]{2,1,0:T(8,128)}), f32[32,40,128]{2,1,0:T(8,128)S(1)}, u32[]{:S(2)}, u32[]{:S(2)}) %all-to-all-start.3) | async-done | bytes 655392 | tf_op jit(solution)/shard_map/all_to_all | solution.py:53
  123.1 0.1 reduce_sum.55
  123.2 0.7 broadcast_in_dim.95
  123.9 8.4 %all-to-all-start.4 = ((f32[16,40,128]{2,1,0:T(8,128)}), f32[16,40,128]{2,1,0:T(8,128)S(1)}, u32[]{:S(2)}, u32[]{:S(2)}) async-start(f32[16,40,128]{2,1,0:T(8,128)} %broadcast_in_dim.95), calls=%async_computation.4 | async-start | bytes 655360 | tf_op jit(solution)/shard_map/all_to_all | solution.py:53
  132.3 0.7 collective-permute-start.6
  133.1 15.8 %all-to-all-done.4 = f32[16,40,128]{2,1,0:T(8,128)S(1)} async-done(((f32[16,40,128]{2,1,0:T(8,128)}), f32[16,40,128]{2,1,0:T(8,128)S(1)}, u32[]{:S(2)}, u32[]{:S(2)}) %all-to-all-start.4) | async-done | bytes 327712 | tf_op jit(solution)/shard_map/all_to_all | solution.py:53
  149.0 0.1 broadcast_in_dim.94
  149.0 1.0 pad_maximum_fusion
  150.0 15.0 %all-to-all-start.5 = ((f32[32,56,128]{2,1,0:T(8,128)}), f32[32,56,128]{2,1,0:T(8,128)S(1)}, u32[]{:S(2)}, u32[]{:S(2)}) async-start(f32[32,56,128]{2,1,0:T(8,128)} %pad_maximum_fusion), calls=%async_computation.5 | async-start | bytes 1835008 | tf_op jit(solution)/shard_map/all_to_all | solution.py:53
  165.1 1.3 collective-permute-start.7
  166.4 3.4 %shard_map.18.refs_2_.refs_3_ = f32[128,128]{1,0:T(8,128)} custom-call(s32[2]{0:T(128)} %pad_add_fusion.refs_0_, f32[128,128]{1,0:T(8,128)} %get-tuple-element.50.refs_1_.refs_4_.refs_9_), custom_call_target="tpu_custom_call" | custom-call | tf_op jit(solution)/shard_map/pallas_call | solution.py:120
  169.8 6.0 %collective-permute-done.7 = f32[128,512]{1,0:T(8,128)S(1)} collective-permute-done((f32[128,512]{1,0:T(8,128)S(1)}, f32[128,512]{1,0:T(8,128)S(1)}, u32[]{:S(2)}, u32[]{:S(2)}) %collective-permute-start.7) | collective-permute-done | bytes 262176 | tf_op jit(solution)/shard_map/ppermute | solution.py:258
  175.8 0.7 add.39.refs_5_
  176.5 4.1 %all-to-all-done.5.refs_1_.refs_2_ = f32[32,56,128]{2,1,0:T(8,128)S(1)} async-done(((f32[32,56,128]{2,1,0:T(8,128)}), f32[32,56,128]{2,1,0:T(8,128)S(1)}, u32[]{:S(2)}, u32[]{:S(2)}) %all-to-all-start.5) | async-done | bytes 917536 | tf_op jit(solution)/shard_map/all_to_all | solution.py:53
  180.6 0.9 copy-done.1
  181.6 4.6 %shard_map.19 = (f32[32,8,128]{2,1,0:T(8,128)}, f32[128,128]{1,0:T(8,128)}, f32[128,128]{1,0:T(8,128)}, f32[512,128]{1,0:T(8,128)}) custom-call(s32[2]{0:T(128)} %pad_add_fusion.refs_0_, f32[32,56,128]{2,1,0:T(8,128)} %copy-done.1, f32[128,128]{1,0:T(8,128)} %shard_map.18.refs_2_.refs_3_, f32[512,128]{1,0:T(8,128)} %get-tuple-element.51.refs_3_.refs_7_, ...), custom_call_target="tpu_custom_call" | custom-call | tf_op jit(solution)/shard_map/pallas_call | solution.py:120
  186.3 1.0 pad_maximum_fusion.3
  187.2 16.7 %all_to_all.55.refs_10_ = f32[32,40,128]{2,1,0:T(8,128)S(1)} all-to-all(f32[32,40,128]{2,1,0:T(8,128)S(1)} %pad_maximum_fusion.3), channel_id=1, replica_groups=mesh['row'=16,'col'=32] {'col'}, dimensions={0} | all-to-all | bytes 1310720 | tf_op jit(solution)/shard_map/all_to_all | solution.py:53
  204.0 0.8 broadcast_in_dim.99
  204.7 3.7 %all-to-all-start.7 = ((f32[32,8,128]{2,1,0:T(8,128)}), f32[32,8,128]{2,1,0:T(8,128)S(1)}, u32[]{:S(2)}, u32[]{:S(2)}) async-start(f32[32,8,128]{2,1,0:T(8,128)} %broadcast_in_dim.99), calls=%async_computation.7 | async-start | bytes 262144 | tf_op jit(solution)/shard_map/all_to_all | solution.py:53
  208.5 6.7 %shard_map.20 = (f32[1024,512]{1,0:T(8,128)}, f32[512,128]{1,0:T(8,128)}, f32[512,128]{1,0:T(8,128)}) custom-call(s32[2]{0:T(128)} %pad_add_fusion.refs_0_, f32[1024,512]{1,0:T(8,128)} %bitcast.53, f32[32,56,128]{2,1,0:T(8,128)} %copy-done.1, f32[128,128]{1,0:T(8,128)} %shard_map.18.refs_2_.refs_3_, f32[128,128]{1,0:T(8,128)} %get-tuple-element.53.refs_4_, ...), custom_call_target="tpu_custom_call" | custom-call | tf_op jit(solution)/shard_map/pallas_call | solution.py:120
  215.2 0.9 all-to-all-done.7
  216.1 0.7 copy-done.4
  216.8 11.7 %shard_map.21 = (f32[32,40,128]{2,1,0:T(8,128)}, f32[512,128]{1,0:T(8,128)}, f32[512,128]{1,0:T(8,128)}, f32[512,128]{1,0:T(8,128)}, f32[128,128]{1,0:T(8,128)}) custom-call(s32[2]{0:T(128)} %pad_add_fusion.refs_0_, f32[256,128]{1,0:T(8,128)} %bitcast.68, f32[512,128]{1,0:T(8,128)} %get-tuple-element.59.refs_2_, f32[512,128]{1,0:T(8,128)} %get-tuple-element.60.refs_3_, ...), custom_call_target="tpu_custom_call" | custom-call | tf_op jit(solution)/shard_map/pallas_call | solution.py:120
  228.5 19.4 %all_to_all.56 = f32[32,40,128]{2,1,0:T(8,128)S(1)} all-to-all(f32[32,40,128]{2,1,0:T(8,128)} %get-tuple-element.62), channel_id=1, replica_groups=mesh['row'=16,'col'=32] {'col'}, dimensions={0} | all-to-all | bytes 1310720 | tf_op jit(solution)/shard_map/all_to_all | solution.py:53
  247.9 0.1 reduce_sum.58
  247.9 0.7 broadcast_in_dim.101
  248.7 7.6 %all-to-all-start.9 = ((f32[16,40,128]{2,1,0:T(8,128)}), f32[16,40,128]{2,1,0:T(8,128)S(1)}, u32[]{:S(2)}, u32[]{:S(2)}) async-start(f32[16,40,128]{2,1,0:T(8,128)} %broadcast_in_dim.101), calls=%async_computation.9 | async-start | bytes 655360 | tf_op jit(solution)/shard_map/all_to_all | solution.py:53
  256.3 17.1 %all-to-all-done.9 = f32[16,40,128]{2,1,0:T(8,128)S(1)} async-done(((f32[16,40,128]{2,1,0:T(8,128)}), f32[16,40,128]{2,1,0:T(8,128)S(1)}, u32[]{:S(2)}, u32[]{:S(2)}) %all-to-all-start.9) | async-done | bytes 327712 | tf_op jit(solution)/shard_map/all_to_all | solution.py:53
  273.4 0.1 broadcast_in_dim.100
  273.5 1.0 pad_maximum_fusion.1
  274.5 8.7 %all-to-all-start.10 = ((f32[32,56,128]{2,1,0:T(8,128)}), f32[32,56,128]{2,1,0:T(8,128)S(1)}, u32[]{:S(2)}, u32[]{:S(2)}) async-start(f32[32,56,128]{2,1,0:T(8,128)} %pad_maximum_fusion.1), calls=%async_computation.10 | async-start | bytes 1835008 | tf_op jit(solution)/shard_map/all_to_all | solution.py:53
  283.2 3.4 %shard_map.22.refs_3_ = f32[128,128]{1,0:T(8,128)} custom-call(s32[2]{0:T(128)} %pad_add_fusion.refs_0_, f32[128,128]{1,0:T(8,128)} %get-tuple-element.63.refs_1_), custom_call_target="tpu_custom_call" | custom-call | tf_op jit(solution)/shard_map/pallas_call | solution.py:120
  286.6 12.2 %all-to-all-done.10.refs_2_ = f32[32,56,128]{2,1,0:T(8,128)S(1)} async-done(((f32[32,56,128]{2,1,0:T(8,128)}), f32[32,56,128]{2,1,0:T(8,128)S(1)}, u32[]{:S(2)}, u32[]{:S(2)}) %all-to-all-start.10) | async-done | bytes 917536 | tf_op jit(solution)/shard_map/all_to_all | solution.py:53
  298.9 0.9 copy-done.2
  299.8 6.2 %shard_map.23 = f32[4096,128]{1,0:T(8,128)} custom-call(s32[2]{0:T(128)} %pad_add_fusion.refs_0_, f32[1024,512]{1,0:T(8,128)} %get-tuple-element.58.refs_5_.refs_1_, f32[32,56,128]{2,1,0:T(8,128)} %copy-done.2, f32[128,128]{1,0:T(8,128)} %shard_map.22.refs_3_, f32[512,128]{1,0:T(8,128)} %get-tuple-element.64.refs_4_, f32[512,128]{1,0:T(8,128)} %get-tuple-element.65.refs_5_, ...), custom_call_target="tpu_custom_call" | custom-call | tf_op jit(solution)/shard_map/pallas_call | solution.py:120
  (40 shorter events, 0.6 us)
Async XLA Ops:
  1.9 2.4 copy-start
  4.2 32.0 %all-to-all-start = ((f32[32,40,128]{2,1,0:T(8,128)}), f32[32,40,128]{2,1,0:T(8,128)S(1)}, u32[]{:S(2)}, u32[]{:S(2)}) async-start(f32[32,40,128]{2,1,0:T(8,128)} %pad_maximum_fusion.2), calls=%async_computation | async-start | bytes 1310720 | tf_op jit(solution)/shard_map/all_to_all | solution.py:53
  17.1 19.0 %collective-permute-start = (f32[128,512]{1,0:T(8,128)S(1)}, f32[128,512]{1,0:T(8,128)S(1)}, u32[]{:S(2)}, u32[]{:S(2)}) collective-permute-start(f32[128,512]{1,0:T(8,128)S(1)} %bitcast.69), channel_id=1, source_target_pairs={{0,256},{1,257},{2,258},{3,259},{4,260},{5,261},{6,262},{7,263},{8... | collective-permute-start | bytes 786440 | tf_op jit(solution)/shard_map/ppermute | solution.py:258
  36.2 14.3 %collective-permute-start.1 = (f32[128,512]{1,0:T(8,128)S(1)}, f32[128,512]{1,0:T(8,128)S(1)}, u32[]{:S(2)}, u32[]{:S(2)}) collective-permute-start(f32[128,512]{1,0:T(8,128)S(1)} %fusion.7), channel_id=1, source_target_pairs={{0,128},{256,384},{1,129},{257,385},{2,130},{258,386},{3,131},{259... | collective-permute-start | bytes 786440 | tf_op jit(solution)/shard_map/ppermute | solution.py:258
  38.2 23.9 %all-to-all-start.1 = ((f32[16,8,128]{2,1,0:T(8,128)}), f32[16,8,128]{2,1,0:T(8,128)S(1)}, u32[]{:S(2)}, u32[]{:S(2)}) async-start(f32[16,8,128]{2,1,0:T(8,128)} %broadcast_in_dim.92), calls=%async_computation.1 | async-start | bytes 131072 | tf_op jit(solution)/shard_map/all_to_all | solution.py:53
  63.0 24.7 %all-to-all-start.2 = ((f32[32,40,128]{2,1,0:T(8,128)}), f32[32,40,128]{2,1,0:T(8,128)S(1)}, u32[]{:S(2)}, u32[]{:S(2)}) async-start(f32[32,40,128]{2,1,0:T(8,128)} %broadcast_in_dim.93), calls=%async_computation.2 | async-start | bytes 1310720 | tf_op jit(solution)/shard_map/all_to_all | solution.py:53
  72.6 8.2 %collective-permute-start.2 = (f32[128,512]{1,0:T(8,128)S(1)}, f32[128,512]{1,0:T(8,128)S(1)}, u32[]{:S(2)}, u32[]{:S(2)}) collective-permute-start(f32[128,512]{1,0:T(8,128)S(1)} %add.33), channel_id=1, source_target_pairs={{0,64},{128,192},{256,320},{384,448},{1,65},{129,193},{257,321},{3... | collective-permute-start | bytes 786440 | tf_op jit(solution)/shard_map/ppermute | solution.py:258
  80.9 6.1 %collective-permute-start.3 = (f32[128,512]{1,0:T(8,128)S(1)}, f32[128,512]{1,0:T(8,128)S(1)}, u32[]{:S(2)}, u32[]{:S(2)}) collective-permute-start(f32[128,512]{1,0:T(8,128)S(1)} %add.34), channel_id=1, source_target_pairs={{0,32},{64,96},{128,160},{192,224},{256,288},{320,352},{384,416},{... | collective-permute-start | bytes 786440 | tf_op jit(solution)/shard_map/ppermute | solution.py:258
  87.7 13.9 %collective-permute-start.4 = (f32[128,512]{1,0:T(8,128)S(1)}, f32[128,512]{1,0:T(8,128)S(1)}, u32[]{:S(2)}, u32[]{:S(2)}) collective-permute-start(f32[128,512]{1,0:T(8,128)S(1)} %bitcast.59), channel_id=1, source_target_pairs={{32,288},{33,289},{34,290},{35,291},{36,292},{37,293},{38,294},{39... | collective-permute-start | bytes 786440 | tf_op jit(solution)/shard_map/ppermute | solution.py:258
  101.7 21.4 %all-to-all-start.3 = ((f32[32,40,128]{2,1,0:T(8,128)}), f32[32,40,128]{2,1,0:T(8,128)S(1)}, u32[]{:S(2)}, u32[]{:S(2)}) async-start(f32[32,40,128]{2,1,0:T(8,128)} %get-tuple-element.43), calls=%async_computation.3 | async-start | bytes 1310720 | tf_op jit(solution)/shard_map/all_to_all | solution.py:53
  110.2 0.7 collective-permute-start.5
  123.9 25.0 %all-to-all-start.4 = ((f32[16,40,128]{2,1,0:T(8,128)}), f32[16,40,128]{2,1,0:T(8,128)S(1)}, u32[]{:S(2)}, u32[]{:S(2)}) async-start(f32[16,40,128]{2,1,0:T(8,128)} %broadcast_in_dim.95), calls=%async_computation.4 | async-start | bytes 655360 | tf_op jit(solution)/shard_map/all_to_all | solution.py:53
  132.3 0.7 collective-permute-start.6
  150.0 30.6 %all-to-all-start.5 = ((f32[32,56,128]{2,1,0:T(8,128)}), f32[32,56,128]{2,1,0:T(8,128)S(1)}, u32[]{:S(2)}, u32[]{:S(2)}) async-start(f32[32,56,128]{2,1,0:T(8,128)} %pad_maximum_fusion), calls=%async_computation.5 | async-start | bytes 1835008 | tf_op jit(solution)/shard_map/all_to_all | solution.py:53
  165.1 10.7 %collective-permute-start.7 = (f32[128,512]{1,0:T(8,128)S(1)}, f32[128,512]{1,0:T(8,128)S(1)}, u32[]{:S(2)}, u32[]{:S(2)}) collective-permute-start(f32[128,512]{1,0:T(8,128)S(1)} %add.38), channel_id=1, source_target_pairs={{32,64},{96,128},{160,192},{224,256},{288,320},{352,384},{416,448}... | collective-permute-start | bytes 786440 | tf_op jit(solution)/shard_map/ppermute | solution.py:258
  180.6 0.9 copy-start.1
  204.0 4.5 %copy-start.3 = (f32[32,40,128]{2,1,0:T(8,128)}, f32[32,40,128]{2,1,0:T(8,128)S(1)}, u32[]{:S(2)}) copy-start(f32[32,40,128]{2,1,0:T(8,128)S(1)} %all_to_all.55.refs_10_) | copy-start | bytes 1966084
  204.7 11.4 %all-to-all-start.7 = ((f32[32,8,128]{2,1,0:T(8,128)}), f32[32,8,128]{2,1,0:T(8,128)S(1)}, u32[]{:S(2)}, u32[]{:S(2)}) async-start(f32[32,8,128]{2,1,0:T(8,128)} %broadcast_in_dim.99), calls=%async_computation.7 | async-start | bytes 262144 | tf_op jit(solution)/shard_map/all_to_all | solution.py:53
  216.1 0.7 copy-start.4
  248.7 24.7 %all-to-all-start.9 = ((f32[16,40,128]{2,1,0:T(8,128)}), f32[16,40,128]{2,1,0:T(8,128)S(1)}, u32[]{:S(2)}, u32[]{:S(2)}) async-start(f32[16,40,128]{2,1,0:T(8,128)} %broadcast_in_dim.101), calls=%async_computation.9 | async-start | bytes 655360 | tf_op jit(solution)/shard_map/all_to_all | solution.py:53
  274.5 24.4 %all-to-all-start.10 = ((f32[32,56,128]{2,1,0:T(8,128)}), f32[32,56,128]{2,1,0:T(8,128)S(1)}, u32[]{:S(2)}, u32[]{:S(2)}) async-start(f32[32,56,128]{2,1,0:T(8,128)} %pad_maximum_fusion.1), calls=%async_computation.10 | async-start | bytes 1835008 | tf_op jit(solution)/shard_map/all_to_all | solution.py:53
  298.9 0.9 copy-start.2

commit v3 on v2

--- a/solution.py
+++ b/solution.py
@@ -144,15 +144,13 @@
         q = dot(keep_from(panel, block, index, first), lower_inverse, 1, 1)
         return first_tile(q, block, lambda tile: tile + identity * jnp.where(index == first, 1.0, 0.0))
 
-    if panel_cols.shape[0] == block:
-        panel_cols = panel_cols.T
     cols = reflect(panel_cols, place[1])
     even = reflect(panel_even, place[0])
     odd = dot(panel_odd, lower_inverse, 1, 1)
     product = wide_dot(current, cols)
     tiles = [product[block * t : block * t + block] for t in range(spread * tile_cols)]
     sums = [jnp.concatenate(tiles[h::spread]) for h in range(spread)]
-    cross = dot(even.T, sums[0]) + dot(odd.T, sums[1])
+    cross = wide_dot(even.T, sums[0]) + wide_dot(odd.T, sums[1])
     if last:
         pivot_rows = jnp.zeros_like(cross)
     else:
@@ -176,14 +174,15 @@
     return [dot(w, inverse_core, 1, 1) - 0.5 * dot(v, core_block) for w, v in pairs]
 
 
-def middle_body(place, got, inverse_core, cols, pivot_tile, next_tile, *, first, sizes):
-    block, spread, part, col_count, small, tile_cols = sizes
-    little = got[:, (spread + 1) * part :].reshape(col_count * small, block)
+def middle_body(place, got, inverse_core, cols, pivot_tile, *, first, sizes):
+    block, spread, part, col_count, small, tile_cols = sizes
+    after = (spread + 1) * part
+    little = got[:, after : after + small].reshape(col_count * small, block)
     core_block = dot(dot(inverse_core, little[:block]), inverse_core, 1, 1)
     w_cols = split_shared(got, 0, sizes)[1]
     companion = dot(w_cols, inverse_core, 1, 1) - 0.5 * dot(cols, core_block)
     companion_tile = dot(little[block:], inverse_core, 1, 1) - 0.5 * dot(pivot_tile, core_block)
-    panel = next_tile.T - (dot(cols, companion_tile, 1, 1) + dot(companion, pivot_tile, 1, 1))
+    panel = got[:, after + small :].reshape(col_count * part, block) - (dot(cols, companion_tile, 1, 1) + dot(companion, pivot_tile, 1, 1))
     masked = keep_from(panel, block, place[1], first + 1)
     gram = dot(masked.T, masked)
     top = panel[:block] * jnp.where(place[1] == first + 1, 1.0, 0.0)
@@ -241,24 +240,15 @@
     def copies_of(value, count):
         return jnp.broadcast_to(value[None], (count,) + value.shape)
 
-    def share(mine, got):
-        wanted = got[:, :chunk].reshape(row_count, spread, part, block)
-        wanted = wanted.transpose(1, 0, 2, 3).reshape(col_count, part, block)
-        total = got[:, chunk:].sum(0)
-        sends = [copies_of(mine[:chunk], col_count), wanted, copies_of(total, col_count)]
+    def share(tall, little):
+        got = exchange(copies_of(jnp.concatenate(tall + [little]), row_count), "row")
+        wanted = []
+        for index in range(len(tall)):
+            piece = got[:, index * chunk : (index + 1) * chunk].reshape(row_count, spread, part, block)
+            wanted.append(piece.transpose(1, 0, 2, 3).reshape(col_count, part, block))
+        total = got[:, len(tall) * chunk :].sum(0)
+        sends = [copies_of(tall[0], col_count), wanted[0], copies_of(total, col_count)] + wanted[1:]
         return exchange(jnp.concatenate(sends, axis=1), "col")
-
-    def only_at(value, source):
-        return jnp.where(row_index == source, value, 0.0)
-
-    def hop(held, source, step):
-        if step >= row_count:
-            return held
-        pairs = [((source + k) % row_count, (source + k + step) % row_count) for k in range(0, row_count, 2 * step)]
-        return held + lax.ppermute(held, "row", pairs)
-
-    def after(value, held):
-        return lax.optimization_barrier((value, held))
 
     current = matrix.reshape(rows, cols)
 
@@ -269,16 +259,11 @@
     top_part = jnp.where(row_index == 1, own_col[:block], 0.0)
     stacked = jnp.concatenate([gram_part, top_part]).reshape(col_count, small, block)
     got = exchange(jnp.concatenate([chunks_of(own_col), stacked], axis=1), "col")
-    got, panel_cols = after(got, hop(only_at(current[:block], 0), 0, 8))
     next_chunk = got[1, :chunk]
-    total = exchange(copies_of(got[0, chunk:], row_count), "row")
-    total, panel_cols = after(total, hop(panel_cols, 0, 4))
-    total = total.sum(0)
-    shared = exchange(copies_of(jnp.concatenate([got[0, :chunk], total]), col_count), "col")
-    panel_cols = hop(hop(panel_cols, 0, 2), 0, 1)
-    shared, next_tile = after(shared, only_at(current[:block], 1))
-    stacked = shared[:, chunk:].reshape(2 * block, block)
+    shared = share([got[0, :chunk]], got[0, chunk:])
+    stacked = shared[:, chunk + part :].reshape(2 * block, block)
     even, odd = (shared[:, part * h : part * h + part].reshape(cols, block) for h in range(spread))
+    panel_cols = shared[:, chunk : chunk + part].reshape(cols, block)
 
     for panel_index in range(2):
         last = panel_index == 1
@@ -289,15 +274,8 @@
             place, stacked, even, odd, panel_cols, current, scratch=tile,
         )
         (inverse_core,) = launch(newton_body, [tile], place, pivot_tile)
-        if last:
-            mine = exchange(send, "col").sum(0)
-            got = share(mine, exchange(copies_of(mine, row_count), "row"))
-        else:
-            send, next_tile = after(send, hop(next_tile, 1, 8))
-            mine, next_tile = after(exchange(send, "col"), hop(next_tile, 1, 4))
-            mine = mine.sum(0)
-            rest, next_tile = after(exchange(copies_of(mine, row_count), "row"), hop(next_tile, 1, 2))
-            got, next_tile = after(share(mine, rest), hop(next_tile, 1, 1))
+        mine = exchange(send, "col").sum(0)
+        got = share([mine[:chunk]] + ([] if last else [next_chunk]), mine[chunk:])
         if last:
             (current,) = launch(
                 functools.partial(final_body, sizes=sizes),
@@ -308,7 +286,7 @@
         send, core_block, companion_tile, next_cols = launch(
             functools.partial(middle_body, first=first, sizes=sizes),
             [(col_count, small, block), tile, tile, tall],
-            place, got, inverse_core, panel_cols, pivot_tile, next_tile,
+            place, got, inverse_core, panel_cols, pivot_tile,
         )
         shared = exchange(jnp.concatenate([copies_of(next_chunk, col_count), send], axis=1), "col")
         total = shared[:, chunk:].sum(0)

time: 307 us -> 298 us (0.971)
  blocking collectives: 36.1 us -> 145 us
  starting transfers between devices: 107 us -> 28.2 us
  waiting for transfers between devices: 94.8 us -> 61.6 us
  other arithmetic: 8.8 us -> 4.91 us
    all_to_all x2 -> x6, blocking collectives: 36.1 us -> 145 us  [exchange(): return lax.all_to_all(chunks, axis, 0, 0)]
    all_to_all x9 -> x5, starting transfers between devices: 84.3 us -> 28.2 us  [exchange(): return lax.all_to_all(chunks, axis, 0, 0)]
    ppermute x8 -> x0, starting transfers between devices: 22.3 us -> none  [hop(): return held + lax.ppermute(held, 'row', pairs)]
    ppermute x8 -> x0, waiting for transfers between devices: 21 us -> none  [hop(): return held + lax.ppermute(held, 'row', pairs)]
    all_to_all x9 -> x5, waiting for transfers between devices: 73.8 us -> 61.6 us  [exchange(): return lax.all_to_all(chunks, axis, 0, 0)]
  transfers between devices with their start and end apart: 17 -> 5, of which waited for: 11 -> 5; matrix products, arithmetic and copies ran while one was open for 2% -> 0% of each run, Pallas kernels for 8% -> 5%
where the time goes in v3:
time: 298 us; the launch traced here: 296 us
  blocking collectives  145 us (49%)
  waiting for transfers between devices  61.6 us (21%)
  Pallas kernels  46.8 us (16%)
  starting transfers between devices  28.2 us (9%)
  local copies, waits for them, and re-layouts  8.13 us (3%)
  other arithmetic  4.91 us (2%)
    all_to_all x6, blocking collectives, exchange(): return lax.all_to_all(chunks, axis, 0, 0)  145 us
    all_to_all x5, waiting for transfers between devices, exchange(): return lax.all_to_all(chunks, axis, 0, 0)  61.6 us
    pallas_call x7, Pallas kernels, launch(): pl.pallas_call(kernel, out_shape=outs, in_specs=[pl.BlockSpec(memory_spac...  46.8 us
    all_to_all x5, starting transfers between devices, exchange(): return lax.all_to_all(chunks, axis, 0, 0)  28.2 us
  transfers between devices with their start and end apart: 5, of which 5 were waited for; matrix products, arithmetic and copies ran while one was open for 0% of the time, Pallas kernels for 5%

profile of v3, /device:TPU:1, one launch (start us, length us, event | category | flops | bytes accessed | tf_op | source)
XLA Modules:
  0.0 296.5 jit_solution(2053459815280467487)
XLA Ops:
  0.0 0.1 broadcast_bitcast_fusion
  0.1 1.8 copy.17
  1.9 0.0 copy-start
  1.9 0.1 slice.83
  1.9 1.3 fusion
  3.3 0.1 copy.9
  3.3 0.0 copy-done
  3.4 22.5 %all_to_all.55 = f32[32,40,128]{2,1,0:T(8,128)S(1)} all-to-all(f32[32,40,128]{2,1,0:T(8,128)S(1)} %pad_maximum_fusion.3), channel_id=1, replica_groups=mesh['row'=16,'col'=32] {'col'}, dimensions={0} | all-to-all | bytes 1310720 | tf_op jit(solution)/shard_map/all_to_all | solution.py:53
  26.0 30.6 %all_to_all.56 = f32[16,40,128]{2,1,0:T(8,128)S(1)} all-to-all(f32[16,40,128]{2,1,0:T(8,128)S(1)} %broadcast_in_dim.48), channel_id=1, replica_groups=mesh['row'=16,'col'=32] {'row'}, dimensions={0} | all-to-all | bytes 655360 | tf_op jit(solution)/shard_map/all_to_all | solution.py:53
  56.6 0.1 broadcast_in_dim.47
  56.7 1.0 pad_maximum_fusion.1
  57.7 8.7 %all-to-all-start.2 = ((f32[32,56,128]{2,1,0:T(8,128)}), f32[32,56,128]{2,1,0:T(8,128)S(1)}, u32[]{:S(2)}, u32[]{:S(2)}) async-start(f32[32,56,128]{2,1,0:T(8,128)} %pad_maximum_fusion.1), calls=%async_computation.2 | async-start | bytes 1835008 | tf_op jit(solution)/shard_map/all_to_all | solution.py:53
  66.4 0.6 pad_add_fusion.refs_0_
  67.0 15.0 %all-to-all-done.2 = f32[32,56,128]{2,1,0:T(8,128)S(1)} async-done(((f32[32,56,128]{2,1,0:T(8,128)}), f32[32,56,128]{2,1,0:T(8,128)S(1)}, u32[]{:S(2)}, u32[]{:S(2)}) %all-to-all-start.2) | async-done | bytes 917536 | tf_op jit(solution)/shard_map/all_to_all | solution.py:53
  82.0 0.7 slice_bitcast_fusion.refs_1_
  82.7 0.9 fusion.6
  83.6 11.2 %shard_map.17 = (f32[32,40,128]{2,1,0:T(8,128)}, f32[512,128]{1,0:T(8,128)}, f32[512,128]{1,0:T(8,128)}, f32[512,128]{1,0:T(8,128)}, f32[128,128]{1,0:T(8,128)}) custom-call(s32[2]{0:T(128)} %pad_add_fusion.refs_0_, f32[256,128]{1,0:T(8,128)} %slice_bitcast_fusion.refs_1_, f32[512,128]{1,0:T(8,128)} %bitcast.62, f32[512,128]{1,0:T(8,128)} %bitcast.61, ...), custom_call_target="tpu_custom_call" | custom-call | tf_op jit(solution)/shard_map/pallas_call | solution.py:120
  94.8 16.8 %all_to_all.57 = f32[32,40,128]{2,1,0:T(8,128)S(1)} all-to-all(f32[32,40,128]{2,1,0:T(8,128)} %get-tuple-element.22), channel_id=1, replica_groups=mesh['row'=16,'col'=32] {'col'}, dimensions={0} | all-to-all | bytes 1310720 | tf_op jit(solution)/shard_map/all_to_all | solution.py:53
  111.6 0.1 reduce_sum.55
  111.7 39.4 %all_to_all.58 = f32[16,72,128]{2,1,0:T(8,128)S(1)} all-to-all(f32[16,72,128]{2,1,0:T(8,128)S(1)} %broadcast_in_dim.51), channel_id=1, replica_groups=mesh['row'=16,'col'=32] {'row'}, dimensions={0} | all-to-all | bytes 1179648 | tf_op jit(solution)/shard_map/all_to_all | solution.py:53
  151.1 0.1 fusion.7
  151.3 0.1 broadcast_in_dim.50
  151.3 1.1 pad_maximum_fusion
  152.4 5.2 %all-to-all-start.5 = ((f32[32,72,128]{2,1,0:T(8,128)}), f32[32,72,128]{2,1,0:T(8,128)S(1)}, u32[]{:S(2)}, u32[]{:S(2)}) async-start(f32[32,72,128]{2,1,0:T(8,128)} %pad_maximum_fusion), calls=%async_computation.5 | async-start | bytes 2359296 | tf_op jit(solution)/shard_map/all_to_all | solution.py:53
  157.7 3.4 %shard_map.18.refs_2_.refs_3_ = f32[128,128]{1,0:T(8,128)} custom-call(s32[2]{0:T(128)} %pad_add_fusion.refs_0_, f32[128,128]{1,0:T(8,128)} %get-tuple-element.23.refs_1_.refs_4_.refs_9_), custom_call_target="tpu_custom_call" | custom-call | tf_op jit(solution)/shard_map/pallas_call | solution.py:120
  161.1 15.0 %all-to-all-done.5.refs_1_.refs_2_ = f32[32,72,128]{2,1,0:T(8,128)S(1)} async-done(((f32[32,72,128]{2,1,0:T(8,128)}), f32[32,72,128]{2,1,0:T(8,128)S(1)}, u32[]{:S(2)}, u32[]{:S(2)}) %all-to-all-start.5) | async-done | bytes 1179680 | tf_op jit(solution)/shard_map/all_to_all | solution.py:53
  176.1 0.0 copy-start.1
  176.1 1.0 copy-done.1
  177.2 4.6 %shard_map.19 = (f32[32,8,128]{2,1,0:T(8,128)}, f32[128,128]{1,0:T(8,128)}, f32[128,128]{1,0:T(8,128)}, f32[512,128]{1,0:T(8,128)}) custom-call(s32[2]{0:T(128)} %pad_add_fusion.refs_0_, f32[32,72,128]{2,1,0:T(8,128)} %copy-done.1, f32[128,128]{1,0:T(8,128)} %shard_map.18.refs_2_.refs_3_, f32[512,128]{1,0:T(8,128)} %get-tuple-element.24.refs_3_.refs_7_, ...), custom_call_target="tpu_custom_call" | custom-call | tf_op jit(solution)/shard_map/pallas_call | solution.py:120
  181.8 1.0 pad_maximum_fusion.4
  182.8 16.6 %all_to_all.59.refs_10_ = f32[32,40,128]{2,1,0:T(8,128)S(1)} all-to-all(f32[32,40,128]{2,1,0:T(8,128)S(1)} %pad_maximum_fusion.4), channel_id=1, replica_groups=mesh['row'=16,'col'=32] {'col'}, dimensions={0} | all-to-all | bytes 1310720 | tf_op jit(solution)/shard_map/all_to_all | solution.py:53
  199.4 0.0 copy-start.3
  199.4 0.8 broadcast_in_dim.97
  200.2 3.7 %all-to-all-start.7 = ((f32[32,8,128]{2,1,0:T(8,128)}), f32[32,8,128]{2,1,0:T(8,128)S(1)}, u32[]{:S(2)}, u32[]{:S(2)}) async-start(f32[32,8,128]{2,1,0:T(8,128)} %broadcast_in_dim.97), calls=%async_computation.7 | async-start | bytes 262144 | tf_op jit(solution)/shard_map/all_to_all | solution.py:53
  203.9 0.0 copy-done.3
  203.9 6.8 %shard_map.20 = (f32[1024,512]{1,0:T(8,128)}, f32[512,128]{1,0:T(8,128)}, f32[512,128]{1,0:T(8,128)}) custom-call(s32[2]{0:T(128)} %pad_add_fusion.refs_0_, f32[1024,512]{1,0:T(8,128)} %bitcast.52, f32[32,72,128]{2,1,0:T(8,128)} %copy-done.1, f32[128,128]{1,0:T(8,128)} %shard_map.18.refs_2_.refs_3_, f32[128,128]{1,0:T(8,128)} %get-tuple-element.25.refs_4_, ...), custom_call_target="tpu_custom_call" | custom-call | tf_op jit(solution)/shard_map/pallas_call | solution.py:120
  210.7 0.9 all-to-all-done.7
  211.5 0.0 copy-start.4
  211.5 0.7 copy-done.4
  212.2 11.2 %shard_map.21 = (f32[32,40,128]{2,1,0:T(8,128)}, f32[512,128]{1,0:T(8,128)}, f32[512,128]{1,0:T(8,128)}, f32[512,128]{1,0:T(8,128)}, f32[128,128]{1,0:T(8,128)}) custom-call(s32[2]{0:T(128)} %pad_add_fusion.refs_0_, f32[256,128]{1,0:T(8,128)} %bitcast.67, f32[512,128]{1,0:T(8,128)} %get-tuple-element.31.refs_2_, f32[512,128]{1,0:T(8,128)} %get-tuple-element.32.refs_3_, ...), custom_call_target="tpu_custom_call" | custom-call | tf_op jit(solution)/shard_map/pallas_call | solution.py:120
  223.4 19.4 %all_to_all.60 = f32[32,40,128]{2,1,0:T(8,128)S(1)} all-to-all(f32[32,40,128]{2,1,0:T(8,128)} %get-tuple-element.34), channel_id=1, replica_groups=mesh['row'=16,'col'=32] {'col'}, dimensions={0} | all-to-all | bytes 1310720 | tf_op jit(solution)/shard_map/all_to_all | solution.py:53
  242.8 0.1 reduce_sum.58
  242.9 0.7 broadcast_in_dim.99
  243.6 3.5 %all-to-all-start.9 = ((f32[16,40,128]{2,1,0:T(8,128)}), f32[16,40,128]{2,1,0:T(8,128)S(1)}, u32[]{:S(2)}, u32[]{:S(2)}) async-start(f32[16,40,128]{2,1,0:T(8,128)} %broadcast_in_dim.99), calls=%async_computation.9 | async-start | bytes 655360 | tf_op jit(solution)/shard_map/all_to_all | solution.py:53
  247.2 18.5 %all-to-all-done.9 = f32[16,40,128]{2,1,0:T(8,128)S(1)} async-done(((f32[16,40,128]{2,1,0:T(8,128)}), f32[16,40,128]{2,1,0:T(8,128)S(1)}, u32[]{:S(2)}, u32[]{:S(2)}) %all-to-all-start.9) | async-done | bytes 327712 | tf_op jit(solution)/shard_map/all_to_all | solution.py:53
  265.8 0.1 broadcast_in_dim.98
  265.9 1.0 pad_maximum_fusion.2
  266.8 7.0 %all-to-all-start.10 = ((f32[32,56,128]{2,1,0:T(8,128)}), f32[32,56,128]{2,1,0:T(8,128)S(1)}, u32[]{:S(2)}, u32[]{:S(2)}) async-start(f32[32,56,128]{2,1,0:T(8,128)} %pad_maximum_fusion.2), calls=%async_computation.10 | async-start | bytes 1835008 | tf_op jit(solution)/shard_map/all_to_all | solution.py:53
  273.8 3.4 %shard_map.22.refs_3_ = f32[128,128]{1,0:T(8,128)} custom-call(s32[2]{0:T(128)} %pad_add_fusion.refs_0_, f32[128,128]{1,0:T(8,128)} %get-tuple-element.35.refs_1_), custom_call_target="tpu_custom_call" | custom-call | tf_op jit(solution)/shard_map/pallas_call | solution.py:120
  277.2 12.1 %all-to-all-done.10.refs_2_ = f32[32,56,128]{2,1,0:T(8,128)S(1)} async-done(((f32[32,56,128]{2,1,0:T(8,128)}), f32[32,56,128]{2,1,0:T(8,128)S(1)}, u32[]{:S(2)}, u32[]{:S(2)}) %all-to-all-start.10) | async-done | bytes 917536 | tf_op jit(solution)/shard_map/all_to_all | solution.py:53
  289.4 0.0 copy-start.2
  289.4 0.9 copy-done.2
  290.3 6.2 %shard_map.23 = f32[4096,128]{1,0:T(8,128)} custom-call(s32[2]{0:T(128)} %pad_add_fusion.refs_0_, f32[1024,512]{1,0:T(8,128)} %get-tuple-element.30.refs_5_.refs_1_, f32[32,56,128]{2,1,0:T(8,128)} %copy-done.2, f32[128,128]{1,0:T(8,128)} %shard_map.22.refs_3_, f32[512,128]{1,0:T(8,128)} %get-tuple-element.36.refs_4_, f32[512,128]{1,0:T(8,128)} %get-tuple-element.37.refs_5_, ...), custom_call_target="tpu_custom_call" | custom-call | tf_op jit(solution)/shard_map/pallas_call | solution.py:120
  (27 shorter events, 0.5 us)
Async XLA Ops:
  1.9 1.5 copy-start
  57.7 24.4 %all-to-all-start.2 = ((f32[32,56,128]{2,1,0:T(8,128)}), f32[32,56,128]{2,1,0:T(8,128)S(1)}, u32[]{:S(2)}, u32[]{:S(2)}) async-start(f32[32,56,128]{2,1,0:T(8,128)} %pad_maximum_fusion.1), calls=%async_computation.2 | async-start | bytes 1835008 | tf_op jit(solution)/shard_map/all_to_all | solution.py:53
  152.4 23.7 %all-to-all-start.5 = ((f32[32,72,128]{2,1,0:T(8,128)}), f32[32,72,128]{2,1,0:T(8,128)S(1)}, u32[]{:S(2)}, u32[]{:S(2)}) async-start(f32[32,72,128]{2,1,0:T(8,128)} %pad_maximum_fusion), calls=%async_computation.5 | async-start | bytes 2359296 | tf_op jit(solution)/shard_map/all_to_all | solution.py:53
  176.1 1.0 copy-start.1
  199.4 4.5 %copy-start.3 = (f32[32,40,128]{2,1,0:T(8,128)}, f32[32,40,128]{2,1,0:T(8,128)S(1)}, u32[]{:S(2)}) copy-start(f32[32,40,128]{2,1,0:T(8,128)S(1)} %all_to_all.59.refs_10_) | copy-start | bytes 1966084
  200.2 11.4 %all-to-all-start.7 = ((f32[32,8,128]{2,1,0:T(8,128)}), f32[32,8,128]{2,1,0:T(8,128)S(1)}, u32[]{:S(2)}, u32[]{:S(2)}) async-start(f32[32,8,128]{2,1,0:T(8,128)} %broadcast_in_dim.97), calls=%async_computation.7 | async-start | bytes 262144 | tf_op jit(solution)/shard_map/all_to_all | solution.py:53
  211.5 0.7 copy-start.4
  243.6 22.1 %all-to-all-start.9 = ((f32[16,40,128]{2,1,0:T(8,128)}), f32[16,40,128]{2,1,0:T(8,128)S(1)}, u32[]{:S(2)}, u32[]{:S(2)}) async-start(f32[16,40,128]{2,1,0:T(8,128)} %broadcast_in_dim.99), calls=%async_computation.9 | async-start | bytes 655360 | tf_op jit(solution)/shard_map/all_to_all | solution.py:53
  266.8 22.5 %all-to-all-start.10 = ((f32[32,56,128]{2,1,0:T(8,128)}), f32[32,56,128]{2,1,0:T(8,128)S(1)}, u32[]{:S(2)}, u32[]{:S(2)}) async-start(f32[32,56,128]{2,1,0:T(8,128)} %pad_maximum_fusion.2), calls=%async_computation.10 | async-start | bytes 1835008 | tf_op jit(solution)/shard_map/all_to_all | solution.py:53
  289.4 0.9 copy-start.2

commit v4 on v2

--- a/solution.py
+++ b/solution.py
@@ -8,7 +8,7 @@
 from jax.sharding import PartitionSpec as P
 
 newton_sweeps = 8
-pivot_group = 4
+pivot_group = 2
 
 
 def dot(left_side, right_side, left_dim=1, right_dim=0):
@@ -144,15 +144,13 @@
         q = dot(keep_from(panel, block, index, first), lower_inverse, 1, 1)
         return first_tile(q, block, lambda tile: tile + identity * jnp.where(index == first, 1.0, 0.0))
 
-    if panel_cols.shape[0] == block:
-        panel_cols = panel_cols.T
     cols = reflect(panel_cols, place[1])
     even = reflect(panel_even, place[0])
     odd = dot(panel_odd, lower_inverse, 1, 1)
     product = wide_dot(current, cols)
     tiles = [product[block * t : block * t + block] for t in range(spread * tile_cols)]
     sums = [jnp.concatenate(tiles[h::spread]) for h in range(spread)]
-    cross = dot(even.T, sums[0]) + dot(odd.T, sums[1])
+    cross = wide_dot(even.T, sums[0]) + wide_dot(odd.T, sums[1])
     if last:
         pivot_rows = jnp.zeros_like(cross)
     else:
@@ -241,15 +239,14 @@
     def copies_of(value, count):
         return jnp.broadcast_to(value[None], (count,) + value.shape)
 
+    def sum_rows(mine):
+        return exchange(copies_of(mine, row_count), "row")
+
     def share(mine, got):
         wanted = got[:, :chunk].reshape(row_count, spread, part, block)
         wanted = wanted.transpose(1, 0, 2, 3).reshape(col_count, part, block)
-        total = got[:, chunk:].sum(0)
-        sends = [copies_of(mine[:chunk], col_count), wanted, copies_of(total, col_count)]
+        sends = [copies_of(mine[:chunk], col_count), wanted, copies_of(got[:, chunk:].sum(0), col_count)]
         return exchange(jnp.concatenate(sends, axis=1), "col")
-
-    def only_at(value, source):
-        return jnp.where(row_index == source, value, 0.0)
 
     def hop(held, source, step):
         if step >= row_count:
@@ -269,16 +266,13 @@
     top_part = jnp.where(row_index == 1, own_col[:block], 0.0)
     stacked = jnp.concatenate([gram_part, top_part]).reshape(col_count, small, block)
     got = exchange(jnp.concatenate([chunks_of(own_col), stacked], axis=1), "col")
-    got, panel_cols = after(got, hop(only_at(current[:block], 0), 0, 8))
     next_chunk = got[1, :chunk]
-    total = exchange(copies_of(got[0, chunk:], row_count), "row")
-    total, panel_cols = after(total, hop(panel_cols, 0, 4))
-    total = total.sum(0)
-    shared = exchange(copies_of(jnp.concatenate([got[0, :chunk], total]), col_count), "col")
-    panel_cols = hop(hop(panel_cols, 0, 2), 0, 1)
-    shared, next_tile = after(shared, only_at(current[:block], 1))
-    stacked = shared[:, chunk:].reshape(2 * block, block)
+    mine = jnp.concatenate([got[0, :chunk], got[0, chunk:]])
+    got, next_tile = after(sum_rows(mine), jnp.where(row_index == 1, current[:block], 0.0))
+    shared, next_tile = after(share(mine, got), hop(next_tile, 1, 8))
+    stacked = shared[:, chunk + part :].reshape(2 * block, block)
     even, odd = (shared[:, part * h : part * h + part].reshape(cols, block) for h in range(spread))
+    panel_cols = shared[:, chunk : chunk + part].reshape(cols, block)
 
     for panel_index in range(2):
         last = panel_index == 1
@@ -291,13 +285,13 @@
         (inverse_core,) = launch(newton_body, [tile], place, pivot_tile)
         if last:
             mine = exchange(send, "col").sum(0)
-            got = share(mine, exchange(copies_of(mine, row_count), "row"))
+            got = share(mine, sum_rows(mine))
         else:
-            send, next_tile = after(send, hop(next_tile, 1, 8))
-            mine, next_tile = after(exchange(send, "col"), hop(next_tile, 1, 4))
+            send, next_tile = after(send, hop(next_tile, 1, 4))
+            mine, next_tile = after(exchange(send, "col"), hop(next_tile, 1, 2))
             mine = mine.sum(0)
-            rest, next_tile = after(exchange(copies_of(mine, row_count), "row"), hop(next_tile, 1, 2))
-            got, next_tile = after(share(mine, rest), hop(next_tile, 1, 1))
+            got, next_tile = after(sum_rows(mine), next_tile)
+            got, next_tile = after(share(mine, got), hop(next_tile, 1, 1))
         if last:
             (current,) = launch(
                 functools.partial(final_body, sizes=sizes),

time: 307 us -> 301 us (0.980)
  starting transfers between devices: 107 us -> 68.9 us
  blocking collectives: 36.1 us -> 59.1 us
  Pallas kernels: 47.8 us -> 54.1 us
  waiting for transfers between devices: 94.8 us -> 99.1 us
    all_to_all x2 -> x3, blocking collectives: 36.1 us -> 59.1 us  [exchange(): return lax.all_to_all(chunks, axis, 0, 0)]
    all_to_all x9 -> x8, starting transfers between devices: 84.3 us -> 65.4 us  [exchange(): return lax.all_to_all(chunks, axis, 0, 0)]
    ppermute x8 -> x4, starting transfers between devices: 22.3 us -> 3.49 us  [hop(): return held + lax.ppermute(held, 'row', pairs)]
    all_to_all x9 -> x8, waiting for transfers between devices: 73.8 us -> 92.6 us  [exchange(): return lax.all_to_all(chunks, axis, 0, 0)]
    ppermute x8 -> x4, waiting for transfers between devices: 21 us -> 6.52 us  [hop(): return held + lax.ppermute(held, 'row', pairs)]
    pallas_call x7, Pallas kernels: 47.8 us -> 54.1 us  [launch(): pl.pallas_call(kernel, out_shape=outs, in_specs=[pl.BlockSpec(memory_spac...]
  transfers between devices with their start and end apart: 17 -> 12, of which waited for: 11 -> 9; matrix products, arithmetic and copies ran while one was open for 2% -> 2% of each run, Pallas kernels for 8% -> 9%
where the time goes in v4:
time: 301 us; the launch traced here: 300 us
  waiting for transfers between devices  99.1 us (33%)
  starting transfers between devices  68.9 us (23%)
  blocking collectives  59.1 us (20%)
  Pallas kernels  54.1 us (18%)
  local copies, waits for them, and re-layouts  9.49 us (3%)
  other arithmetic  7.36 us (2%)
    all_to_all x8, waiting for transfers between devices, exchange(): return lax.all_to_all(chunks, axis, 0, 0)  92.6 us
    all_to_all x8, starting transfers between devices, exchange(): return lax.all_to_all(chunks, axis, 0, 0)  65.4 us
    all_to_all x3, blocking collectives, exchange(): return lax.all_to_all(chunks, axis, 0, 0)  59.1 us
    pallas_call x7, Pallas kernels, launch(): pl.pallas_call(kernel, out_shape=outs, in_specs=[pl.BlockSpec(memory_spac...  54.1 us
    ppermute x4, waiting for transfers between devices, hop(): return held + lax.ppermute(held, 'row', pairs)  6.52 us
  transfers between devices with their start and end apart: 12, of which 9 were waited for; matrix products, arithmetic and copies ran while one was open for 2% of the time, Pallas kernels for 9%

profile of v4, /device:TPU:1, one launch (start us, length us, event | category | flops | bytes accessed | tf_op | source)
XLA Modules:
  0.0 299.8 jit_solution(4936117425030725655)
XLA Ops:
  0.0 0.1 broadcast_bitcast_fusion
  0.1 1.8 copy.17
  1.9 0.0 copy-start
  1.9 0.1 slice.78
  1.9 1.3 fusion
  3.3 0.1 copy.8
  3.4 0.0 copy-done
  3.4 22.5 %all_to_all.55 = f32[32,40,128]{2,1,0:T(8,128)S(1)} all-to-all(f32[32,40,128]{2,1,0:T(8,128)S(1)} %pad_maximum_fusion.3), channel_id=1, replica_groups=mesh['row'=16,'col'=32] {'col'}, dimensions={0} | all-to-all | bytes 1310720 | tf_op jit(solution)/shard_map/all_to_all | solution.py:53
  25.9 0.8 broadcast_in_dim.54
  26.7 13.7 %all-to-all-start.1 = ((f32[16,40,128]{2,1,0:T(8,128)}), f32[16,40,128]{2,1,0:T(8,128)S(1)}, u32[]{:S(2)}, u32[]{:S(2)}) async-start(f32[16,40,128]{2,1,0:T(8,128)} %broadcast_in_dim.54), calls=%async_computation.1 | async-start | bytes 655360 | tf_op jit(solution)/shard_map/all_to_all | solution.py:53
  40.4 1.7 fusion.2
  42.2 15.3 %all-to-all-done.1 = f32[16,40,128]{2,1,0:T(8,128)S(1)} async-done(((f32[16,40,128]{2,1,0:T(8,128)}), f32[16,40,128]{2,1,0:T(8,128)S(1)}, u32[]{:S(2)}, u32[]{:S(2)}) %all-to-all-start.1) | async-done | bytes 327712 | tf_op jit(solution)/shard_map/all_to_all | solution.py:53
  57.6 0.1 broadcast_in_dim.53
  57.6 1.0 pad_maximum_fusion
  58.6 8.7 %all-to-all-start.2 = ((f32[32,56,128]{2,1,0:T(8,128)}), f32[32,56,128]{2,1,0:T(8,128)S(1)}, u32[]{:S(2)}, u32[]{:S(2)}) async-start(f32[32,56,128]{2,1,0:T(8,128)} %pad_maximum_fusion), calls=%async_computation.2 | async-start | bytes 1835008 | tf_op jit(solution)/shard_map/all_to_all | solution.py:53
  67.3 0.7 collective-permute-start
  68.0 0.6 pad_add_fusion.refs_0_
  68.6 0.0 collective-permute-done
  68.6 14.3 %all-to-all-done.2 = f32[32,56,128]{2,1,0:T(8,128)S(1)} async-done(((f32[32,56,128]{2,1,0:T(8,128)}), f32[32,56,128]{2,1,0:T(8,128)S(1)}, u32[]{:S(2)}, u32[]{:S(2)}) %all-to-all-start.2) | async-done | bytes 917536 | tf_op jit(solution)/shard_map/all_to_all | solution.py:53
  83.0 0.7 collective-permute-start.1
  83.7 0.7 slice_bitcast_fusion.refs_1_
  84.3 0.9 fusion.7
  85.3 14.9 %shard_map.17 = (f32[32,40,128]{2,1,0:T(8,128)}, f32[512,128]{1,0:T(8,128)}, f32[512,128]{1,0:T(8,128)}, f32[512,128]{1,0:T(8,128)}, f32[128,128]{1,0:T(8,128)}) custom-call(s32[2]{0:T(128)} %pad_add_fusion.refs_0_, f32[256,128]{1,0:T(8,128)} %slice_bitcast_fusion.refs_1_, f32[512,128]{1,0:T(8,128)} %bitcast.64, f32[512,128]{1,0:T(8,128)} %bitcast.63, ...), custom_call_target="tpu_custom_call" | custom-call | tf_op jit(solution)/shard_map/pallas_call | solution.py:120
  100.2 0.0 collective-permute-done.1
  100.2 3.9 %all-to-all-start.3 = ((f32[32,40,128]{2,1,0:T(8,128)}), f32[32,40,128]{2,1,0:T(8,128)S(1)}, u32[]{:S(2)}, u32[]{:S(2)}) async-start(f32[32,40,128]{2,1,0:T(8,128)} %get-tuple-element.39), calls=%async_computation.3 | async-start | bytes 1310720 | tf_op jit(solution)/shard_map/all_to_all | solution.py:53
  104.1 0.7 collective-permute-start.2
  104.8 0.0 collective-permute-done.2
  104.8 12.2 %all-to-all-done.3 = f32[32,40,128]{2,1,0:T(8,128)S(1)} async-done(((f32[32,40,128]{2,1,0:T(8,128)}), f32[32,40,128]{2,1,0:T(8,128)S(1)}, u32[]{:S(2)}, u32[]{:S(2)}) %all-to-all-start.3) | async-done | bytes 655392 | tf_op jit(solution)/shard_map/all_to_all | solution.py:53
  117.0 0.1 reduce_sum.55
  117.1 0.8 broadcast_in_dim.101
  117.8 13.0 %all-to-all-start.4 = ((f32[16,40,128]{2,1,0:T(8,128)}), f32[16,40,128]{2,1,0:T(8,128)S(1)}, u32[]{:S(2)}, u32[]{:S(2)}) async-start(f32[16,40,128]{2,1,0:T(8,128)} %broadcast_in_dim.101), calls=%async_computation.4 | async-start | bytes 655360 | tf_op jit(solution)/shard_map/all_to_all | solution.py:53
  130.8 17.1 %all-to-all-done.4 = f32[16,40,128]{2,1,0:T(8,128)S(1)} async-done(((f32[16,40,128]{2,1,0:T(8,128)}), f32[16,40,128]{2,1,0:T(8,128)S(1)}, u32[]{:S(2)}, u32[]{:S(2)}) %all-to-all-start.4) | async-done | bytes 327712 | tf_op jit(solution)/shard_map/all_to_all | solution.py:53
  148.0 0.1 broadcast_in_dim.100
  148.0 1.0 pad_maximum_fusion.1
  149.0 8.7 %all-to-all-start.5 = ((f32[32,56,128]{2,1,0:T(8,128)}), f32[32,56,128]{2,1,0:T(8,128)S(1)}, u32[]{:S(2)}, u32[]{:S(2)}) async-start(f32[32,56,128]{2,1,0:T(8,128)} %pad_maximum_fusion.1), calls=%async_computation.5 | async-start | bytes 1835008 | tf_op jit(solution)/shard_map/all_to_all | solution.py:53
  157.7 1.5 collective-permute-start.3
  159.2 3.4 %shard_map.18.refs_2_.refs_3_ = f32[128,128]{1,0:T(8,128)} custom-call(s32[2]{0:T(128)} %pad_add_fusion.refs_0_, f32[128,128]{1,0:T(8,128)} %get-tuple-element.46.refs_1_.refs_4_.refs_9_), custom_call_target="tpu_custom_call" | custom-call | tf_op jit(solution)/shard_map/pallas_call | solution.py:120
  162.6 6.5 %collective-permute-done.3 = f32[128,512]{1,0:T(8,128)S(1)} collective-permute-done((f32[128,512]{1,0:T(8,128)S(1)}, f32[128,512]{1,0:T(8,128)S(1)}, u32[]{:S(2)}, u32[]{:S(2)}) %collective-permute-start.3) | collective-permute-done | bytes 262176 | tf_op jit(solution)/shard_map/ppermute | solution.py:255
  169.1 0.7 add.23.refs_5_
  169.9 3.5 %all-to-all-done.5.refs_1_.refs_2_ = f32[32,56,128]{2,1,0:T(8,128)S(1)} async-done(((f32[32,56,128]{2,1,0:T(8,128)}), f32[32,56,128]{2,1,0:T(8,128)S(1)}, u32[]{:S(2)}, u32[]{:S(2)}) %all-to-all-start.5) | async-done | bytes 917536 | tf_op jit(solution)/shard_map/all_to_all | solution.py:53
  173.4 0.0 copy-start.1
  173.4 1.0 copy-done.1
  174.3 4.7 %shard_map.19 = (f32[32,8,128]{2,1,0:T(8,128)}, f32[128,128]{1,0:T(8,128)}, f32[128,128]{1,0:T(8,128)}, f32[512,128]{1,0:T(8,128)}) custom-call(s32[2]{0:T(128)} %pad_add_fusion.refs_0_, f32[32,56,128]{2,1,0:T(8,128)} %copy-done.1, f32[128,128]{1,0:T(8,128)} %shard_map.18.refs_2_.refs_3_, f32[512,128]{1,0:T(8,128)} %get-tuple-element.47.refs_3_.refs_7_, ...), custom_call_target="tpu_custom_call" | custom-call | tf_op jit(solution)/shard_map/pallas_call | solution.py:120
  179.1 1.0 pad_maximum_fusion.4
  180.0 17.2 %all_to_all.56.refs_10_ = f32[32,40,128]{2,1,0:T(8,128)S(1)} all-to-all(f32[32,40,128]{2,1,0:T(8,128)S(1)} %pad_maximum_fusion.4), channel_id=1, replica_groups=mesh['row'=16,'col'=32] {'col'}, dimensions={0} | all-to-all | bytes 1310720 | tf_op jit(solution)/shard_map/all_to_all | solution.py:53
  197.3 0.7 broadcast_in_dim.105
  198.0 3.7 %all-to-all-start.7 = ((f32[32,8,128]{2,1,0:T(8,128)}), f32[32,8,128]{2,1,0:T(8,128)S(1)}, u32[]{:S(2)}, u32[]{:S(2)}) async-start(f32[32,8,128]{2,1,0:T(8,128)} %broadcast_in_dim.105), calls=%async_computation.7 | async-start | bytes 262144 | tf_op jit(solution)/shard_map/all_to_all | solution.py:53
  201.7 0.0 copy-done.3
  201.7 6.7 %shard_map.20 = (f32[1024,512]{1,0:T(8,128)}, f32[512,128]{1,0:T(8,128)}, f32[512,128]{1,0:T(8,128)}) custom-call(s32[2]{0:T(128)} %pad_add_fusion.refs_0_, f32[1024,512]{1,0:T(8,128)} %bitcast.52, f32[32,56,128]{2,1,0:T(8,128)} %copy-done.1, f32[128,128]{1,0:T(8,128)} %shard_map.18.refs_2_.refs_3_, f32[128,128]{1,0:T(8,128)} %get-tuple-element.49.refs_4_, ...), custom_call_target="tpu_custom_call" | custom-call | tf_op jit(solution)/shard_map/pallas_call | solution.py:120
  208.5 0.9 all-to-all-done.7
  209.4 0.7 copy-done.4
  210.1 14.9 %shard_map.21 = (f32[32,40,128]{2,1,0:T(8,128)}, f32[512,128]{1,0:T(8,128)}, f32[512,128]{1,0:T(8,128)}, f32[512,128]{1,0:T(8,128)}, f32[128,128]{1,0:T(8,128)}) custom-call(s32[2]{0:T(128)} %pad_add_fusion.refs_0_, f32[256,128]{1,0:T(8,128)} %bitcast.68, f32[512,128]{1,0:T(8,128)} %get-tuple-element.55.refs_2_, f32[512,128]{1,0:T(8,128)} %get-tuple-element.56.refs_3_, ...), custom_call_target="tpu_custom_call" | custom-call | tf_op jit(solution)/shard_map/pallas_call | solution.py:120
  225.0 19.3 %all_to_all.57 = f32[32,40,128]{2,1,0:T(8,128)S(1)} all-to-all(f32[32,40,128]{2,1,0:T(8,128)} %get-tuple-element.58), channel_id=1, replica_groups=mesh['row'=16,'col'=32] {'col'}, dimensions={0} | all-to-all | bytes 1310720 | tf_op jit(solution)/shard_map/all_to_all | solution.py:53
  244.3 0.1 reduce_sum.58
  244.4 0.7 broadcast_in_dim.107
  245.1 4.9 %all-to-all-start.9 = ((f32[16,40,128]{2,1,0:T(8,128)}), f32[16,40,128]{2,1,0:T(8,128)S(1)}, u32[]{:S(2)}, u32[]{:S(2)}) async-start(f32[16,40,128]{2,1,0:T(8,128)} %broadcast_in_dim.107), calls=%async_computation.9 | async-start | bytes 655360 | tf_op jit(solution)/shard_map/all_to_all | solution.py:53
  250.1 17.1 %all-to-all-done.9 = f32[16,40,128]{2,1,0:T(8,128)S(1)} async-done(((f32[16,40,128]{2,1,0:T(8,128)}), f32[16,40,128]{2,1,0:T(8,128)S(1)}, u32[]{:S(2)}, u32[]{:S(2)}) %all-to-all-start.9) | async-done | bytes 327712 | tf_op jit(solution)/shard_map/all_to_all | solution.py:53
  267.2 0.1 broadcast_in_dim.106
  267.3 1.0 pad_maximum_fusion.2
  268.2 8.7 %all-to-all-start.10 = ((f32[32,56,128]{2,1,0:T(8,128)}), f32[32,56,128]{2,1,0:T(8,128)S(1)}, u32[]{:S(2)}, u32[]{:S(2)}) async-start(f32[32,56,128]{2,1,0:T(8,128)} %pad_maximum_fusion.2), calls=%async_computation.10 | async-start | bytes 1835008 | tf_op jit(solution)/shard_map/all_to_all | solution.py:53
  277.0 3.4 %shard_map.22.refs_3_ = f32[128,128]{1,0:T(8,128)} custom-call(s32[2]{0:T(128)} %pad_add_fusion.refs_0_, f32[128,128]{1,0:T(8,128)} %get-tuple-element.59.refs_1_), custom_call_target="tpu_custom_call" | custom-call | tf_op jit(solution)/shard_map/pallas_call | solution.py:120
  280.4 12.2 %all-to-all-done.10.refs_2_ = f32[32,56,128]{2,1,0:T(8,128)S(1)} async-done(((f32[32,56,128]{2,1,0:T(8,128)}), f32[32,56,128]{2,1,0:T(8,128)S(1)}, u32[]{:S(2)}, u32[]{:S(2)}) %all-to-all-start.10) | async-done | bytes 917536 | tf_op jit(solution)/shard_map/all_to_all | solution.py:53
  292.6 1.0 copy-done.2
  293.6 6.2 %shard_map.23 = f32[4096,128]{1,0:T(8,128)} custom-call(s32[2]{0:T(128)} %pad_add_fusion.refs_0_, f32[1024,512]{1,0:T(8,128)} %get-tuple-element.54.refs_5_.refs_1_, f32[32,56,128]{2,1,0:T(8,128)} %copy-done.2, f32[128,128]{1,0:T(8,128)} %shard_map.22.refs_3_, f32[512,128]{1,0:T(8,128)} %get-tuple-element.60.refs_4_, f32[512,128]{1,0:T(8,128)} %get-tuple-element.61.refs_5_, ...), custom_call_target="tpu_custom_call" | custom-call | tf_op jit(solution)/shard_map/pallas_call | solution.py:120
  (30 shorter events, 0.5 us)
Async XLA Ops:
  1.9 1.6 copy-start
  26.7 30.8 %all-to-all-start.1 = ((f32[16,40,128]{2,1,0:T(8,128)}), f32[16,40,128]{2,1,0:T(8,128)S(1)}, u32[]{:S(2)}, u32[]{:S(2)}) async-start(f32[16,40,128]{2,1,0:T(8,128)} %broadcast_in_dim.54), calls=%async_computation.1 | async-start | bytes 655360 | tf_op jit(solution)/shard_map/all_to_all | solution.py:53
  58.6 24.4 %all-to-all-start.2 = ((f32[32,56,128]{2,1,0:T(8,128)}), f32[32,56,128]{2,1,0:T(8,128)S(1)}, u32[]{:S(2)}, u32[]{:S(2)}) async-start(f32[32,56,128]{2,1,0:T(8,128)} %pad_maximum_fusion), calls=%async_computation.2 | async-start | bytes 1835008 | tf_op jit(solution)/shard_map/all_to_all | solution.py:53
  67.3 1.3 collective-permute-start
  83.0 17.2 %collective-permute-start.1 = (f32[128,512]{1,0:T(8,128)S(1)}, f32[128,512]{1,0:T(8,128)S(1)}, u32[]{:S(2)}, u32[]{:S(2)}) collective-permute-start(f32[128,512]{1,0:T(8,128)S(1)} %add.20), channel_id=1, source_target_pairs={{32,160},{288,416},{33,161},{289,417},{34,162},{290,418},{35,163},... | collective-permute-start | bytes 786440 | tf_op jit(solution)/shard_map/ppermute | solution.py:255
  100.2 16.8 %all-to-all-start.3 = ((f32[32,40,128]{2,1,0:T(8,128)}), f32[32,40,128]{2,1,0:T(8,128)S(1)}, u32[]{:S(2)}, u32[]{:S(2)}) async-start(f32[32,40,128]{2,1,0:T(8,128)} %get-tuple-element.39), calls=%async_computation.3 | async-start | bytes 1310720 | tf_op jit(solution)/shard_map/all_to_all | solution.py:53
  104.1 0.7 collective-permute-start.2
  117.8 30.0 %all-to-all-start.4 = ((f32[16,40,128]{2,1,0:T(8,128)}), f32[16,40,128]{2,1,0:T(8,128)S(1)}, u32[]{:S(2)}, u32[]{:S(2)}) async-start(f32[16,40,128]{2,1,0:T(8,128)} %broadcast_in_dim.101), calls=%async_computation.4 | async-start | bytes 655360 | tf_op jit(solution)/shard_map/all_to_all | solution.py:53
  149.0 24.4 %all-to-all-start.5 = ((f32[32,56,128]{2,1,0:T(8,128)}), f32[32,56,128]{2,1,0:T(8,128)S(1)}, u32[]{:S(2)}, u32[]{:S(2)}) async-start(f32[32,56,128]{2,1,0:T(8,128)} %pad_maximum_fusion.1), calls=%async_computation.5 | async-start | bytes 1835008 | tf_op jit(solution)/shard_map/all_to_all | solution.py:53
  157.7 11.4 %collective-permute-start.3 = (f32[128,512]{1,0:T(8,128)S(1)}, f32[128,512]{1,0:T(8,128)S(1)}, u32[]{:S(2)}, u32[]{:S(2)}) collective-permute-start(f32[128,512]{1,0:T(8,128)S(1)} %add.22), channel_id=1, source_target_pairs={{32,64},{96,128},{160,192},{224,256},{288,320},{352,384},{416,448}... | collective-permute-start | bytes 786440 | tf_op jit(solution)/shard_map/ppermute | solution.py:255
  173.4 1.0 copy-start.1
  197.2 4.5 %copy-start.3 = (f32[32,40,128]{2,1,0:T(8,128)}, f32[32,40,128]{2,1,0:T(8,128)S(1)}, u32[]{:S(2)}) copy-start(f32[32,40,128]{2,1,0:T(8,128)S(1)} %all_to_all.56.refs_10_) | copy-start | bytes 1966084
  198.0 11.4 %all-to-all-start.7 = ((f32[32,8,128]{2,1,0:T(8,128)}), f32[32,8,128]{2,1,0:T(8,128)S(1)}, u32[]{:S(2)}, u32[]{:S(2)}) async-start(f32[32,8,128]{2,1,0:T(8,128)} %broadcast_in_dim.105), calls=%async_computation.7 | async-start | bytes 262144 | tf_op jit(solution)/shard_map/all_to_all | solution.py:53
  209.4 0.7 copy-start.4
  245.1 22.0 %all-to-all-start.9 = ((f32[16,40,128]{2,1,0:T(8,128)}), f32[16,40,128]{2,1,0:T(8,128)S(1)}, u32[]{:S(2)}, u32[]{:S(2)}) async-start(f32[16,40,128]{2,1,0:T(8,128)} %broadcast_in_dim.107), calls=%async_computation.9 | async-start | bytes 655360 | tf_op jit(solution)/shard_map/all_to_all | solution.py:53
  268.2 24.4 %all-to-all-start.10 = ((f32[32,56,128]{2,1,0:T(8,128)}), f32[32,56,128]{2,1,0:T(8,128)S(1)}, u32[]{:S(2)}, u32[]{:S(2)}) async-start(f32[32,56,128]{2,1,0:T(8,128)} %pad_maximum_fusion.2), calls=%async_computation.10 | async-start | bytes 1835008 | tf_op jit(solution)/shard_map/all_to_all | solution.py:53
  292.6 1.0 copy-start.2

commit v5 on v4

--- a/solution.py
+++ b/solution.py
@@ -8,7 +8,7 @@
 from jax.sharding import PartitionSpec as P
 
 newton_sweeps = 8
-pivot_group = 2
+pivot_group = 8
 
 
 def dot(left_side, right_side, left_dim=1, right_dim=0):
@@ -101,13 +101,18 @@
     return scratch[...]
 
 
-def launch(body, shapes, place, *operands, scratch=None, lines=None):
+def launch(body, shapes, place, *operands, scratch=None, lines=None, split=None):
     outs = [jax.ShapeDtypeStruct(shape, jnp.float32) for shape in shapes]
 
     def kernel(*refs):
         extra = refs[len(refs) - 1 :] if scratch else ()
         inputs = refs[1 : 1 + len(operands)]
-        results = body(refs[0], *[ref[...] for ref in inputs], *extra)
+        values = [ref[...] for ref in inputs[1 if split else 0 :]]
+        if split:
+            count = inputs[0].shape[0] // split
+            runs = [inputs[0][pl.ds(u, count, stride=split), :] for u in range(split)]
+            values.insert(0, jnp.concatenate(runs, axis=1))
+        results = body(refs[0], *values, *extra)
         for ref, value in zip(refs[1 + len(operands) : 1 + len(operands) + len(outs)], results, strict=True):
             if lines:
                 width = value.shape[1] // lines
@@ -160,6 +165,24 @@
     return send, even, odd, cols, pivot_tile
 
 
+def pack_body(place, current, *, sizes):
+    block, spread, part, col_count, small, tile_cols = sizes
+    own = current[:, :block]
+    masked = keep_from(own, block, place[0], 1)
+    top = own[:block] * jnp.where(place[0] == 1, 1.0, 0.0)
+    little = jnp.concatenate([dot(masked.T, masked), top]).reshape(col_count, small, block)
+    tiles = [own[block * t : block * t + block] for t in range(spread * tile_cols)]
+    sums = [jnp.concatenate(tiles[h::spread]) for h in range(spread)]
+    return current, jnp.concatenate([each.reshape(col_count, part, block) for each in sums] + [little], axis=1)
+
+
+def opening_body(place, shared, current, scratch, *, first, last, sizes):
+    block, spread, part, col_count, small, tile_cols = sizes
+    (even, odd), cols = split_shared(shared, 0, sizes)
+    stacked = shared[:, (spread + 1) * part :].reshape(col_count * small, block)
+    return front_body(place, stacked, even, odd, cols, current, scratch, first=first, last=last, sizes=sizes)
+
+
 def split_shared(got, start, sizes):
     block, spread, part, col_count, small, tile_cols = sizes
     pieces = [
@@ -232,10 +255,6 @@
     tall = (cols, block)
     tile = (block, block)
 
-    def chunks_of(values):
-        split = values.reshape(tile_cols, spread, block // part, part, block)
-        return split.transpose(0, 2, 1, 3, 4).reshape(col_count, chunk, block)
-
     def copies_of(value, count):
         return jnp.broadcast_to(value[None], (count,) + value.shape)
 
@@ -257,30 +276,25 @@
     def after(value, held):
         return lax.optimization_barrier((value, held))
 
-    current = matrix.reshape(rows, cols)
-
-    own_col = current[:, :block]
-    tile_ids = jnp.repeat(jnp.arange(tile_rows, dtype=jnp.int32) * row_count + row_index, block)[:, None]
-    masked = jnp.where(tile_ids >= 1, own_col, 0.0)
-    gram_part = dot(masked, masked, 0, 0)
-    top_part = jnp.where(row_index == 1, own_col[:block], 0.0)
-    stacked = jnp.concatenate([gram_part, top_part]).reshape(col_count, small, block)
-    got = exchange(jnp.concatenate([chunks_of(own_col), stacked], axis=1), "col")
+    current, send = launch(
+        functools.partial(pack_body, sizes=sizes),
+        [(rows, cols), (col_count, chunk + small, block)],
+        place, matrix.reshape(rows * tile_cols, block), split=tile_cols,
+    )
+    got = exchange(send, "col")
     next_chunk = got[1, :chunk]
     mine = jnp.concatenate([got[0, :chunk], got[0, chunk:]])
     got, next_tile = after(sum_rows(mine), jnp.where(row_index == 1, current[:block], 0.0))
     shared, next_tile = after(share(mine, got), hop(next_tile, 1, 8))
-    stacked = shared[:, chunk + part :].reshape(2 * block, block)
-    even, odd = (shared[:, part * h : part * h + part].reshape(cols, block) for h in range(spread))
-    panel_cols = shared[:, chunk : chunk + part].reshape(cols, block)
+    opening = [shared]
 
     for panel_index in range(2):
         last = panel_index == 1
         first = panel_index + 1
         send, even, odd, panel_cols, pivot_tile = launch(
-            functools.partial(front_body, first=first, last=last, sizes=sizes),
+            functools.partial(front_body if last else opening_body, first=first, last=last, sizes=sizes),
             [(col_count, chunk + small, block), tall, tall, tall, tile],
-            place, stacked, even, odd, panel_cols, current, scratch=tile,
+            place, *opening, current, scratch=tile,
         )
         (inverse_core,) = launch(newton_body, [tile], place, pivot_tile)
         if last:
@@ -312,7 +326,7 @@
             [(rows, cols), tall, tall],
             place, current, got, inverse_core, core_block, even, odd, panel_cols, companion_tile, pivot_tile, shared,
         )
-        panel_cols = next_cols
+        opening = [stacked, even, odd, next_cols]
     return current.reshape(matrix.shape)
 
 

time: 301 us -> 292 us (0.970)
  Pallas kernels: 54.1 us -> 49 us
  local copies, waits for them, and re-layouts: 9.49 us -> 6.1 us
    pallas_call x7 -> x8, Pallas kernels: 54.1 us -> 49 us  [launch(): pl.pallas_call(kernel, out_shape=outs, in_specs=[pl.BlockSpec(memory_spac...]
  transfers between devices with their start and end apart: 12 -> 12, of which waited for: 9 -> 9; matrix products, arithmetic and copies ran while one was open for 2% -> 1% of each run, Pallas kernels for 9% -> 8%
where the time goes in v5:
time: 292 us; the launch traced here: 290 us
  waiting for transfers between devices  100 us (34%)
  starting transfers between devices  67.9 us (23%)
  blocking collectives  60 us (21%)
  Pallas kernels  49 us (17%)
  other arithmetic  6.6 us (2%)
  local copies, waits for them, and re-layouts  6.1 us (2%)
    all_to_all x8, waiting for transfers between devices, exchange(): return lax.all_to_all(chunks, axis, 0, 0)  94 us
    all_to_all x8, starting transfers between devices, exchange(): return lax.all_to_all(chunks, axis, 0, 0)  64.5 us
    all_to_all x3, blocking collectives, exchange(): return lax.all_to_all(chunks, axis, 0, 0)  60 us
    pallas_call x8, Pallas kernels, launch(): pl.pallas_call(kernel, out_shape=outs, in_specs=[pl.BlockSpec(memory_spac...  49 us
    ppermute x4, waiting for transfers between devices, hop(): return held + lax.ppermute(held, 'row', pairs)  6.53 us
  transfers between devices with their start and end apart: 12, of which 9 were waited for; matrix products, arithmetic and copies ran while one was open for 1% of the time, Pallas kernels for 8%

profile of v5, /device:TPU:1, one launch (start us, length us, event | category | flops | bytes accessed | tf_op | source)
XLA Modules:
  0.0 290.4 jit_solution(4948835957841348558)
XLA Ops:
  0.0 0.7 pad_add_fusion.refs_0_
  0.7 3.9 %shard_map.17 = (f32[1024,512]{1,0:T(8,128)}, f32[32,40,128]{2,1,0:T(8,128)}) custom-call(s32[2]{0:T(128)} %pad_add_fusion.refs_0_, f32[4096,128]{1,0:T(8,128)} %bitcast.25), custom_call_target="tpu_custom_call" | custom-call | tf_op jit(solution)/shard_map/pallas_call | solution.py:125
  4.5 23.4 %all_to_all.55 = f32[32,40,128]{2,1,0:T(8,128)S(1)} all-to-all(f32[32,40,128]{2,1,0:T(8,128)} %get-tuple-element.37), channel_id=1, replica_groups=mesh['row'=16,'col'=32] {'col'}, dimensions={0} | all-to-all | bytes 1310720 | tf_op jit(solution)/shard_map/all_to_all | solution.py:53
  27.9 0.7 broadcast_in_dim.32
  28.7 13.0 %all-to-all-start.1 = ((f32[16,40,128]{2,1,0:T(8,128)}), f32[16,40,128]{2,1,0:T(8,128)S(1)}, u32[]{:S(2)}, u32[]{:S(2)}) async-start(f32[16,40,128]{2,1,0:T(8,128)} %broadcast_in_dim.32), calls=%async_computation.1 | async-start | bytes 655360 | tf_op jit(solution)/shard_map/all_to_all | solution.py:53
  41.7 1.0 slice_select_fusion
  42.7 16.1 %all-to-all-done.1 = f32[16,40,128]{2,1,0:T(8,128)S(1)} async-done(((f32[16,40,128]{2,1,0:T(8,128)}), f32[16,40,128]{2,1,0:T(8,128)S(1)}, u32[]{:S(2)}, u32[]{:S(2)}) %all-to-all-start.1) | async-done | bytes 327712 | tf_op jit(solution)/shard_map/all_to_all | solution.py:53
  58.8 0.1 broadcast_in_dim.31
  58.9 1.0 pad_maximum_fusion
  59.9 8.7 %all-to-all-start.2 = ((f32[32,56,128]{2,1,0:T(8,128)}), f32[32,56,128]{2,1,0:T(8,128)S(1)}, u32[]{:S(2)}, u32[]{:S(2)}) async-start(f32[32,56,128]{2,1,0:T(8,128)} %pad_maximum_fusion), calls=%async_computation.2 | async-start | bytes 1835008 | tf_op jit(solution)/shard_map/all_to_all | solution.py:53
  68.6 0.7 collective-permute-start
  69.3 0.0 collective-permute-done
  69.4 14.9 %all-to-all-done.2.refs_1_ = f32[32,56,128]{2,1,0:T(8,128)S(1)} async-done(((f32[32,56,128]{2,1,0:T(8,128)}), f32[32,56,128]{2,1,0:T(8,128)S(1)}, u32[]{:S(2)}, u32[]{:S(2)}) %all-to-all-start.2) | async-done | bytes 917536 | tf_op jit(solution)/shard_map/all_to_all | solution.py:53
  84.3 0.0 copy-start.2
  84.3 0.7 collective-permute-start.1
  84.9 0.2 copy-done.2
  85.2 10.4 %shard_map.18 = (f32[32,40,128]{2,1,0:T(8,128)}, f32[512,128]{1,0:T(8,128)}, f32[512,128]{1,0:T(8,128)}, f32[512,128]{1,0:T(8,128)}, f32[128,128]{1,0:T(8,128)}) custom-call(s32[2]{0:T(128)} %pad_add_fusion.refs_0_, f32[32,56,128]{2,1,0:T(8,128)} %copy-done.2, f32[1024,512]{1,0:T(8,128)} %get-tuple-element.36.refs_2_.refs_1_), custom_call_target="tpu_custom_call" | custom-call | tf_op jit(solution)/shard_map/pallas_call | solution.py:125
  95.6 0.0 collective-permute-done.1
  95.6 3.9 %all-to-all-start.3 = ((f32[32,40,128]{2,1,0:T(8,128)}), f32[32,40,128]{2,1,0:T(8,128)S(1)}, u32[]{:S(2)}, u32[]{:S(2)}) async-start(f32[32,40,128]{2,1,0:T(8,128)} %get-tuple-element.43), calls=%async_computation.3 | async-start | bytes 1310720 | tf_op jit(solution)/shard_map/all_to_all | solution.py:53
  99.5 0.7 collective-permute-start.2
  100.2 0.0 collective-permute-done.2
  100.3 12.2 %all-to-all-done.3 = f32[32,40,128]{2,1,0:T(8,128)S(1)} async-done(((f32[32,40,128]{2,1,0:T(8,128)}), f32[32,40,128]{2,1,0:T(8,128)S(1)}, u32[]{:S(2)}, u32[]{:S(2)}) %all-to-all-start.3) | async-done | bytes 655392 | tf_op jit(solution)/shard_map/all_to_all | solution.py:53
  112.4 0.1 reduce_sum.55
  112.5 0.7 broadcast_in_dim.36
  113.2 12.8 %all-to-all-start.4 = ((f32[16,40,128]{2,1,0:T(8,128)}), f32[16,40,128]{2,1,0:T(8,128)S(1)}, u32[]{:S(2)}, u32[]{:S(2)}) async-start(f32[16,40,128]{2,1,0:T(8,128)} %broadcast_in_dim.36), calls=%async_computation.4 | async-start | bytes 655360 | tf_op jit(solution)/shard_map/all_to_all | solution.py:53
  126.0 17.1 %all-to-all-done.4 = f32[16,40,128]{2,1,0:T(8,128)S(1)} async-done(((f32[16,40,128]{2,1,0:T(8,128)}), f32[16,40,128]{2,1,0:T(8,128)S(1)}, u32[]{:S(2)}, u32[]{:S(2)}) %all-to-all-start.4) | async-done | bytes 327712 | tf_op jit(solution)/shard_map/all_to_all | solution.py:53
  143.2 0.1 broadcast_in_dim.35
  143.2 1.0 pad_maximum_fusion.1
  144.2 8.7 %all-to-all-start.5 = ((f32[32,56,128]{2,1,0:T(8,128)}), f32[32,56,128]{2,1,0:T(8,128)S(1)}, u32[]{:S(2)}, u32[]{:S(2)}) async-start(f32[32,56,128]{2,1,0:T(8,128)} %pad_maximum_fusion.1), calls=%async_computation.5 | async-start | bytes 1835008 | tf_op jit(solution)/shard_map/all_to_all | solution.py:53
  152.9 1.5 collective-permute-start.3
  154.4 3.4 %shard_map.19.refs_2_.refs_3_ = f32[128,128]{1,0:T(8,128)} custom-call(s32[2]{0:T(128)} %pad_add_fusion.refs_0_, f32[128,128]{1,0:T(8,128)} %get-tuple-element.50.refs_1_.refs_4_.refs_9_), custom_call_target="tpu_custom_call" | custom-call | tf_op jit(solution)/shard_map/pallas_call | solution.py:125
  157.8 6.5 %collective-permute-done.3 = f32[128,512]{1,0:T(8,128)S(1)} collective-permute-done((f32[128,512]{1,0:T(8,128)S(1)}, f32[128,512]{1,0:T(8,128)S(1)}, u32[]{:S(2)}, u32[]{:S(2)}) %collective-permute-start.3) | collective-permute-done | bytes 262176 | tf_op jit(solution)/shard_map/ppermute | solution.py:274
  164.3 0.7 add.15.refs_5_
  165.1 3.5 %all-to-all-done.5.refs_1_.refs_2_ = f32[32,56,128]{2,1,0:T(8,128)S(1)} async-done(((f32[32,56,128]{2,1,0:T(8,128)}), f32[32,56,128]{2,1,0:T(8,128)S(1)}, u32[]{:S(2)}, u32[]{:S(2)}) %all-to-all-start.5) | async-done | bytes 917536 | tf_op jit(solution)/shard_map/all_to_all | solution.py:53
  168.6 0.0 copy-start
  168.6 0.9 copy-done
  169.5 4.6 %shard_map.20 = (f32[32,8,128]{2,1,0:T(8,128)}, f32[128,128]{1,0:T(8,128)}, f32[128,128]{1,0:T(8,128)}, f32[512,128]{1,0:T(8,128)}) custom-call(s32[2]{0:T(128)} %pad_add_fusion.refs_0_, f32[32,56,128]{2,1,0:T(8,128)} %copy-done, f32[128,128]{1,0:T(8,128)} %shard_map.19.refs_2_.refs_3_, f32[512,128]{1,0:T(8,128)} %get-tuple-element.51.refs_3_.refs_7_, ...), custom_call_target="tpu_custom_call" | custom-call | tf_op jit(solution)/shard_map/pallas_call | solution.py:125
  174.2 1.0 pad_maximum_fusion.3
  175.2 17.2 %all_to_all.56.refs_10_ = f32[32,40,128]{2,1,0:T(8,128)S(1)} all-to-all(f32[32,40,128]{2,1,0:T(8,128)S(1)} %pad_maximum_fusion.3), channel_id=1, replica_groups=mesh['row'=16,'col'=32] {'col'}, dimensions={0} | all-to-all | bytes 1310720 | tf_op jit(solution)/shard_map/all_to_all | solution.py:53
  192.4 0.0 copy-start.3
  192.4 0.7 broadcast_in_dim.40
  193.2 3.7 %all-to-all-start.7 = ((f32[32,8,128]{2,1,0:T(8,128)}), f32[32,8,128]{2,1,0:T(8,128)S(1)}, u32[]{:S(2)}, u32[]{:S(2)}) async-start(f32[32,8,128]{2,1,0:T(8,128)} %broadcast_in_dim.40), calls=%async_computation.7 | async-start | bytes 262144 | tf_op jit(solution)/shard_map/all_to_all | solution.py:53
  196.9 0.0 copy-done.3
  196.9 6.7 %shard_map.21 = (f32[1024,512]{1,0:T(8,128)}, f32[512,128]{1,0:T(8,128)}, f32[512,128]{1,0:T(8,128)}) custom-call(s32[2]{0:T(128)} %pad_add_fusion.refs_0_, f32[1024,512]{1,0:T(8,128)} %get-tuple-element.36.refs_2_.refs_1_, f32[32,56,128]{2,1,0:T(8,128)} %copy-done, f32[128,128]{1,0:T(8,128)} %shard_map.19.refs_2_.refs_3_, ...), custom_call_target="tpu_custom_call" | custom-call | tf_op jit(solution)/shard_map/pallas_call | solution.py:125
  203.6 1.0 all-to-all-done.7
  204.6 0.0 copy-start.4
  204.6 0.7 copy-done.4
  205.2 10.4 %shard_map.22 = (f32[32,40,128]{2,1,0:T(8,128)}, f32[512,128]{1,0:T(8,128)}, f32[512,128]{1,0:T(8,128)}, f32[512,128]{1,0:T(8,128)}, f32[128,128]{1,0:T(8,128)}) custom-call(s32[2]{0:T(128)} %pad_add_fusion.refs_0_, f32[256,128]{1,0:T(8,128)} %bitcast.32, f32[512,128]{1,0:T(8,128)} %get-tuple-element.59.refs_2_, f32[512,128]{1,0:T(8,128)} %get-tuple-element.60.refs_3_, ...), custom_call_target="tpu_custom_call" | custom-call | tf_op jit(solution)/shard_map/pallas_call | solution.py:125
  215.6 19.3 %all_to_all.57 = f32[32,40,128]{2,1,0:T(8,128)S(1)} all-to-all(f32[32,40,128]{2,1,0:T(8,128)} %get-tuple-element.62), channel_id=1, replica_groups=mesh['row'=16,'col'=32] {'col'}, dimensions={0} | all-to-all | bytes 1310720 | tf_op jit(solution)/shard_map/all_to_all | solution.py:53
  235.0 0.1 reduce_sum.58
  235.0 0.7 broadcast_in_dim.42
  235.8 4.9 %all-to-all-start.9 = ((f32[16,40,128]{2,1,0:T(8,128)}), f32[16,40,128]{2,1,0:T(8,128)S(1)}, u32[]{:S(2)}, u32[]{:S(2)}) async-start(f32[16,40,128]{2,1,0:T(8,128)} %broadcast_in_dim.42), calls=%async_computation.9 | async-start | bytes 655360 | tf_op jit(solution)/shard_map/all_to_all | solution.py:53
  240.7 17.1 %all-to-all-done.9 = f32[16,40,128]{2,1,0:T(8,128)S(1)} async-done(((f32[16,40,128]{2,1,0:T(8,128)}), f32[16,40,128]{2,1,0:T(8,128)S(1)}, u32[]{:S(2)}, u32[]{:S(2)}) %all-to-all-start.9) | async-done | bytes 327712 | tf_op jit(solution)/shard_map/all_to_all | solution.py:53
  257.9 0.1 broadcast_in_dim.41
  257.9 1.0 pad_maximum_fusion.2
  258.9 8.7 %all-to-all-start.10 = ((f32[32,56,128]{2,1,0:T(8,128)}), f32[32,56,128]{2,1,0:T(8,128)S(1)}, u32[]{:S(2)}, u32[]{:S(2)}) async-start(f32[32,56,128]{2,1,0:T(8,128)} %pad_maximum_fusion.2), calls=%async_computation.10 | async-start | bytes 1835008 | tf_op jit(solution)/shard_map/all_to_all | solution.py:53
  267.6 3.4 %shard_map.23.refs_3_ = f32[128,128]{1,0:T(8,128)} custom-call(s32[2]{0:T(128)} %pad_add_fusion.refs_0_, f32[128,128]{1,0:T(8,128)} %get-tuple-element.63.refs_1_), custom_call_target="tpu_custom_call" | custom-call | tf_op jit(solution)/shard_map/pallas_call | solution.py:125
  271.0 12.2 %all-to-all-done.10.refs_2_ = f32[32,56,128]{2,1,0:T(8,128)S(1)} async-done(((f32[32,56,128]{2,1,0:T(8,128)}), f32[32,56,128]{2,1,0:T(8,128)S(1)}, u32[]{:S(2)}, u32[]{:S(2)}) %all-to-all-start.10) | async-done | bytes 917536 | tf_op jit(solution)/shard_map/all_to_all | solution.py:53
  283.3 0.0 copy-start.1
  283.3 0.9 copy-done.1
  284.2 6.2 %shard_map.24 = f32[4096,128]{1,0:T(8,128)} custom-call(s32[2]{0:T(128)} %pad_add_fusion.refs_0_, f32[1024,512]{1,0:T(8,128)} %get-tuple-element.58.refs_5_.refs_1_, f32[32,56,128]{2,1,0:T(8,128)} %copy-done.1, f32[128,128]{1,0:T(8,128)} %shard_map.23.refs_3_, f32[512,128]{1,0:T(8,128)} %get-tuple-element.64.refs_4_, f32[512,128]{1,0:T(8,128)} %get-tuple-element.65.refs_5_, ...), custom_call_target="tpu_custom_call" | custom-call | tf_op jit(solution)/shard_map/pallas_call | solution.py:125
  (22 shorter events, 0.4 us)
Async XLA Ops:
  28.7 30.1 %all-to-all-start.1 = ((f32[16,40,128]{2,1,0:T(8,128)}), f32[16,40,128]{2,1,0:T(8,128)S(1)}, u32[]{:S(2)}, u32[]{:S(2)}) async-start(f32[16,40,128]{2,1,0:T(8,128)} %broadcast_in_dim.32), calls=%async_computation.1 | async-start | bytes 655360 | tf_op jit(solution)/shard_map/all_to_all | solution.py:53
  59.9 24.4 %all-to-all-start.2 = ((f32[32,56,128]{2,1,0:T(8,128)}), f32[32,56,128]{2,1,0:T(8,128)S(1)}, u32[]{:S(2)}, u32[]{:S(2)}) async-start(f32[32,56,128]{2,1,0:T(8,128)} %pad_maximum_fusion), calls=%async_computation.2 | async-start | bytes 1835008 | tf_op jit(solution)/shard_map/all_to_all | solution.py:53
  68.6 0.7 collective-permute-start
  84.3 0.9 copy-start.2
  84.3 11.3 %collective-permute-start.1 = (f32[128,512]{1,0:T(8,128)S(1)}, f32[128,512]{1,0:T(8,128)S(1)}, u32[]{:S(2)}, u32[]{:S(2)}) collective-permute-start(f32[128,512]{1,0:T(8,128)S(1)} %add.12), channel_id=1, source_target_pairs={{32,160},{288,416},{33,161},{289,417},{34,162},{290,418},{35,163},... | collective-permute-start | bytes 786440 | tf_op jit(solution)/shard_map/ppermute | solution.py:274
  95.6 16.8 %all-to-all-start.3 = ((f32[32,40,128]{2,1,0:T(8,128)}), f32[32,40,128]{2,1,0:T(8,128)S(1)}, u32[]{:S(2)}, u32[]{:S(2)}) async-start(f32[32,40,128]{2,1,0:T(8,128)} %get-tuple-element.43), calls=%async_computation.3 | async-start | bytes 1310720 | tf_op jit(solution)/shard_map/all_to_all | solution.py:53
  99.5 0.7 collective-permute-start.2
  113.2 29.8 %all-to-all-start.4 = ((f32[16,40,128]{2,1,0:T(8,128)}), f32[16,40,128]{2,1,0:T(8,128)S(1)}, u32[]{:S(2)}, u32[]{:S(2)}) async-start(f32[16,40,128]{2,1,0:T(8,128)} %broadcast_in_dim.36), calls=%async_computation.4 | async-start | bytes 655360 | tf_op jit(solution)/shard_map/all_to_all | solution.py:53
  144.2 24.4 %all-to-all-start.5 = ((f32[32,56,128]{2,1,0:T(8,128)}), f32[32,56,128]{2,1,0:T(8,128)S(1)}, u32[]{:S(2)}, u32[]{:S(2)}) async-start(f32[32,56,128]{2,1,0:T(8,128)} %pad_maximum_fusion.1), calls=%async_computation.5 | async-start | bytes 1835008 | tf_op jit(solution)/shard_map/all_to_all | solution.py:53
  152.9 11.4 %collective-permute-start.3 = (f32[128,512]{1,0:T(8,128)S(1)}, f32[128,512]{1,0:T(8,128)S(1)}, u32[]{:S(2)}, u32[]{:S(2)}) collective-permute-start(f32[128,512]{1,0:T(8,128)S(1)} %add.14), channel_id=1, source_target_pairs={{32,64},{96,128},{160,192},{224,256},{288,320},{352,384},{416,448}... | collective-permute-start | bytes 786440 | tf_op jit(solution)/shard_map/ppermute | solution.py:274
  168.6 0.9 copy-start
  192.4 4.5 %copy-start.3 = (f32[32,40,128]{2,1,0:T(8,128)}, f32[32,40,128]{2,1,0:T(8,128)S(1)}, u32[]{:S(2)}) copy-start(f32[32,40,128]{2,1,0:T(8,128)S(1)} %all_to_all.56.refs_10_) | copy-start | bytes 1966084
  193.2 11.4 %all-to-all-start.7 = ((f32[32,8,128]{2,1,0:T(8,128)}), f32[32,8,128]{2,1,0:T(8,128)S(1)}, u32[]{:S(2)}, u32[]{:S(2)}) async-start(f32[32,8,128]{2,1,0:T(8,128)} %broadcast_in_dim.40), calls=%async_computation.7 | async-start | bytes 262144 | tf_op jit(solution)/shard_map/all_to_all | solution.py:53
  204.6 0.7 copy-start.4
  235.8 22.0 %all-to-all-start.9 = ((f32[16,40,128]{2,1,0:T(8,128)}), f32[16,40,128]{2,1,0:T(8,128)S(1)}, u32[]{:S(2)}, u32[]{:S(2)}) async-start(f32[16,40,128]{2,1,0:T(8,128)} %broadcast_in_dim.42), calls=%async_computation.9 | async-start | bytes 655360 | tf_op jit(solution)/shard_map/all_to_all | solution.py:53
  258.9 24.4 %all-to-all-start.10 = ((f32[32,56,128]{2,1,0:T(8,128)}), f32[32,56,128]{2,1,0:T(8,128)S(1)}, u32[]{:S(2)}, u32[]{:S(2)}) async-start(f32[32,56,128]{2,1,0:T(8,128)} %pad_maximum_fusion.2), calls=%async_computation.10 | async-start | bytes 1835008 | tf_op jit(solution)/shard_map/all_to_all | solution.py:53
  283.3 0.9 copy-start.1
